TPU v7x, 256 devices: a whole 4x4x8 slice. The times are simulated.
256 devices in a mesh: dp: 32 (over z, y_lo, core), space: 8 (over x, y_hi).
Axes of the slice: x: 4, y: 4 (y_hi: 2, y_lo: 2; y = y_hi * 2 + y_lo), z: 8, core: 2. Of those that a mesh axis runs over, the one named last changes fastest.
Arguments:
- occupancy: int32 [32, 5, 128, 128], P('dp', None, 'space'), may hold values from 0 to 8191
- state_labels: int32 [32, 8, 8], P('dp', 'space'), may hold values 0 or 1
- lift_weight: bfloat16 [13, 32], replicated, may hold values from -1.75 to 1.75
- temporal_weight: bfloat16 [3, 3, 5, 32, 64], replicated, may hold values from -0.21875 to 0.21875
- middle_weight: bfloat16 [3, 3, 64, 128], replicated, may hold values from -0.375 to 0.375
- deeper_weight: bfloat16 [3, 3, 128, 256], replicated, may hold values from -0.25 to 0.25
- deepest_weight: bfloat16 [3, 3, 256, 512], replicated, may hold values from -0.1875 to 0.1875
- head_weight: bfloat16 [512], replicated, may hold values from -0.25 to 0.25
Outputs:
- temporal_grad: float32 [3, 3, 5, 32, 64], replicated
- middle_grad: float32 [3, 3, 64, 128], replicated
- deeper_grad: float32 [3, 3, 128, 256], replicated
- deepest_grad: float32 [3, 3, 256, 512], replicated
- head_grad: float32 [512], replicated
All inputs are finite; a program needn't handle non-finite values. No bound on the sum of `state_labels` on one device may be relied on, other than what follows from the above.
Results may differ from a plain program's by a relative error of at most 0.015.
Values may be sent and summed in bfloat16 or wider, within the bound.
A program may use at most 64 MiB of HBM per device.

v0:
```python
import jax
import jax.numpy as jnp
from jax import lax
from jax.sharding import PartitionSpec as P


def from_behind(block, axis, distance):
    devices = range(lax.axis_size(axis))
    route = [(i - distance, i) for i in devices if i - distance in devices]
    return lax.ppermute(block, axis, route)


def conv_layer(feature_map, weight):
    upper_row = from_behind(feature_map[:, :, -1:, :], "space", 1)
    padded = jnp.concatenate([upper_row, feature_map], axis=2)
    padded = jnp.pad(padded, ((0, 0), (0, 0), (0, 0), (1, 0)))
    accumulated = lax.conv_general_dilated(
        padded,
        weight,
        (2, 2),
        "VALID",
        dimension_numbers=("NCHW", "HWIO", "NCHW"),
        preferred_element_type=jnp.float32,
    )
    gate = jax.nn.sigmoid(accumulated)
    slope = gate * (1.0 + accumulated * (1.0 - gate))
    return ((accumulated * gate).astype(jnp.bfloat16), slope, padded)


def weight_grad(padded, delta):
    return lax.conv_general_dilated(
        padded,
        delta,
        (1, 1),
        "VALID",
        rhs_dilation=(2, 2),
        dimension_numbers=("CNHW", "IOHW", "HWNC"),
        preferred_element_type=jnp.float32,
    )


def input_grad(delta, weight):
    flipped = weight[::-1, ::-1]
    accumulated = lax.conv_general_dilated(
        delta,
        flipped,
        (1, 1),
        ((2, 2), (2, 2)),
        lhs_dilation=(2, 2),
        dimension_numbers=("NCHW", "HWOI", "NCHW"),
        preferred_element_type=jnp.float32,
    )
    lower_row = from_behind(accumulated[:, :, 0:1, 1:], "space", -1)
    local_part = accumulated[:, :, 1:, 1:]
    return jnp.concatenate([local_part[:, :, :-1], local_part[:, :, -1:] + lower_row], axis=2)


def local(
    occupancy,
    state_labels,
    lift_weight,
    temporal_weight,
    middle_weight,
    deeper_weight,
    deepest_weight,
    head_weight,
):
    samples_here = occupancy.shape[0]
    frames = occupancy.shape[1]
    heights = lift_weight.shape[0]
    lift_width = lift_weight.shape[1]
    shifts = jnp.arange(heights, dtype=jnp.int32)
    height_bits = jnp.bitwise_and(
        jnp.right_shift(occupancy[:, :, None], shifts[None, None, :, None, None]), 1
    ).astype(jnp.bfloat16)
    lifted = jnp.einsum(
        "stcrw,ck->stkrw", height_bits, lift_weight, preferred_element_type=jnp.float32
    )
    lifted = jnp.maximum(lifted, 0.0).astype(jnp.bfloat16)
    lifted = lifted.reshape(samples_here, frames * lift_width, lifted.shape[3], lifted.shape[4])
    first_kernel = temporal_weight.reshape(3, 3, frames * lift_width, temporal_weight.shape[4])
    first_map, first_slope, lifted_padded = conv_layer(lifted, first_kernel)
    second_map, second_slope, first_padded = conv_layer(first_map, middle_weight)
    third_map, third_slope, second_padded = conv_layer(second_map, deeper_weight)
    fourth_map, fourth_slope, third_padded = conv_layer(third_map, deepest_weight)
    batch_total = state_labels.shape[0] * lax.axis_size("dp")
    logits = jnp.einsum("sorw,o->srw", fourth_map, head_weight, preferred_element_type=jnp.float32)
    logit_grad = (jax.nn.sigmoid(logits) - state_labels.astype(jnp.float32)) / batch_total
    head_float = head_weight.astype(jnp.float32)
    head_grad = jnp.einsum("sorw,srw->o", fourth_map.astype(jnp.float32), logit_grad)
    fourth_delta = (logit_grad[:, None] * head_float[None, :, None, None] * fourth_slope).astype(
        jnp.bfloat16
    )
    deepest_grad = weight_grad(third_padded, fourth_delta)
    third_delta = (input_grad(fourth_delta, deepest_weight) * third_slope).astype(jnp.bfloat16)
    deeper_grad = weight_grad(second_padded, third_delta)
    second_delta = (input_grad(third_delta, deeper_weight) * second_slope).astype(jnp.bfloat16)
    middle_grad = weight_grad(first_padded, second_delta)
    first_delta = (input_grad(second_delta, middle_weight) * first_slope).astype(jnp.bfloat16)
    temporal_grad = weight_grad(lifted_padded, first_delta).reshape(temporal_weight.shape)
    reduced = lax.psum(
        (temporal_grad, middle_grad, deeper_grad, deepest_grad, head_grad), ("dp", "space")
    )
    return (reduced[0], reduced[1], reduced[2], reduced[3], reduced[4])


def solution(mesh):
    return jax.shard_map(
        local,
        mesh=mesh,
        in_specs=(
            P("dp", None, "space", None),
            P("dp", "space", None),
            P(),
            P(),
            P(),
            P(),
            P(),
            P(),
        ),
        out_specs=(P(), P(), P(), P(), P()),
        check_vma=False,
    )
```

profile of v0, /device:TPU:1, one launch (start us, length us, event | category | flops | bytes accessed | tf_op | source)
XLA Modules:
  0.0 402.3 jit_solution(4823248896462357719)
XLA Ops:
  7.2 1.3 fusion.9
  8.8 2.8 copy.146
  11.6 1.0 slice.81
  12.7 5.6 %collective-permute-start = (bf16[1,160,1,128]{1,0,3,2:T(2,128)(2,1)S(1)}, bf16[1,160,1,128]{1,0,3,2:T(2,128)(2,1)S(1)}, u32[]{:S(2)}, u32[]{:S(2)}) collective-permute-start(bf16[1,160,1,128]{1,0,3,2:T(2,128)(2,1)S(1)} %slice.81), channel_id=1, source_target_pairs={{0,1},{1,2},{2,3},{3,4},{4,5},{5,6},{6,7},{8,9},{9,10},{10,11},{11... | collective-permute-start | bytes 122888 | tf_op jit(solution)/shard_map/ppermute | solution.py:10
  18.3 2.2 collective-permute-done
  20.5 6.2 %pad_maximum_fusion = bf16[1,160,17,128]{1,0,3,2:T(2,128)(2,1)} fusion(bf16[1,160,16,128]{1,0,3,2:T(2,128)(2,1)} %copy.146, bf16[1,160,1,128]{1,0,3,2:T(2,128)(2,1)S(1)} %collective-permute-done), kind=kLoop, calls=%fused_computation.2 | loop fusion | flops 348160 | bytes 1392640 | tf_op jit(solution)/shard_map/concatenate | solution.py:15
  26.7 5.9 %copy.148 = bf16[1,160,17,128]{3,1,2,0:T(8,128)(2,1)} copy(bf16[1,160,17,128]{1,0,3,2:T(2,128)(2,1)} %pad_maximum_fusion) | data formatting | bytes 1392640 | tf_op jit(solution)/shard_map/concatenate | solution.py:15
  32.7 1.7 copy.200
  34.3 1.5 pad.8.clone
  35.8 3.4 reshape.106
  39.2 1.8 copy.151
  41.1 1.6 add_multiply_fusion
  42.7 5.6 %collective-permute-start.1 = (bf16[1,64,1,64]{1,0,3,2:T(2,128)(2,1)S(1)}, bf16[1,64,1,64]{1,0,3,2:T(2,128)(2,1)S(1)}, u32[]{:S(2)}, u32[]{:S(2)}) collective-permute-start(bf16[1,64,1,64]{1,0,3,2:T(2,128)(2,1)S(1)} %slice_bitcast_fusion.1), channel_id=1, source_target_pairs={{0,1},{1,2},{2,3},{3,4},{4,5},{5,6},{6,7},{8,9},{9,10},{10,11},{11... | collective-permute-start | bytes 24584 | tf_op jit(solution)/shard_map/ppermute | solution.py:10
  50.4 1.9 add_multiply_fusion.1
  52.4 5.2 %collective-permute-start.2 = (bf16[1,128,1,32]{1,0,3,2:T(2,128)(2,1)S(1)}, bf16[1,128,1,32]{1,0,3,2:T(2,128)(2,1)S(1)}, u32[]{:S(2)}, u32[]{:S(2)}) collective-permute-start(bf16[1,128,1,32]{1,0,3,2:T(2,128)(2,1)S(1)} %slice_bitcast_fusion.3), channel_id=1, source_target_pairs={{0,1},{1,2},{2,3},{3,4},{4,5},{5,6},{6,7},{8,9},{9,10},{10,11},{11... | collective-permute-start | bytes 24584 | tf_op jit(solution)/shard_map/ppermute | solution.py:10
  59.4 5.1 %collective-permute-start.3 = (bf16[1,256,1,16]{1,0,3,2:T(2,128)(2,1)S(1)}, bf16[1,256,1,16]{1,0,3,2:T(2,128)(2,1)S(1)}, u32[]{:S(2)}, u32[]{:S(2)}) collective-permute-start(bf16[1,256,1,16]{1,0,3,2:T(2,128)(2,1)S(1)} %slice_bitcast_fusion.2), channel_id=1, source_target_pairs={{0,1},{1,2},{2,3},{3,4},{4,5},{5,6},{6,7},{8,9},{9,10},{10,11},{11... | collective-permute-start | bytes 24584 | tf_op jit(solution)/shard_map/ppermute | solution.py:10
  64.6 1.0 copy.184
  68.8 1.5 collective-permute-start.4
  70.3 3.1 fusion.62
  73.3 2.2 collective-permute-done.4
  76.0 1.4 collective-permute-start.5
  77.4 1.5 fusion.85
  79.0 4.1 %collective-permute-done.5 = f32[1,128,1,32]{1,0,3,2:T(1,128)S(1)} collective-permute-done((f32[1,128,1,32]{1,0,3,2:T(1,128)S(1)}, f32[1,128,1,32]{1,0,3,2:T(1,128)S(1)}, u32[]{:S(2)}, u32[]{:S(2)}) %collective-permute-start.5) | collective-permute-done | bytes 16416 | tf_op jit(solution)/shard_map/ppermute | solution.py:10
  83.8 1.4 collective-permute-start.6
  85.3 2.5 fusion.93
  87.8 3.3 collective-permute-done.6
  91.1 5.6 %fusion.25 = f32[3,3,160,64]{3,2,1,0:T(8,128)} fusion(bf16[1,160,17,128]{1,0,3,2:T(2,128)(2,1)S(1)} %copy-done.1, bf16[1,64,8,64]{1,3,2,0:T(8,128)(2,1)S(1)} %fusion.24), kind=kOutput, calls=%fused_computation.40 | convolution fusion | flops 93880320 | bytes 1130496 | tf_op jit(solution)/shard_map/conv_general_dilated | solution.py:31
  97.5 88.2 %psum.39 = f32[512]{0:T(512)} all-reduce(f32[512]{0:T(512)S(1)} %bitcast.187), channel_id=1, replica_groups=mesh['dp'=32,'space'=8] {'dp','space'}, use_global_device_ids=true, to_apply=%region_4.5 | all-reduce | flops 512 | bytes 4096 | tf_op jit(solution)/shard_map/psum | solution.py:101
  185.7 199.9 %all-reduce.3.cloned.1.call-done = (f32[3,3,5,32,64]{4,3,2,1,0:T(8,128)}, f32[3,3,64,128]{3,2,1,0:T(8,128)}, f32[3,3,128,256]{3,2,1,0:T(8,128)}, f32[3,3,256,512]{3,2,1,0:T(8,128)}) async-done(((f32[3,3,5,32,64]{4,3,2,1,0:T(8,128)}, f32[3,3,64,128]{3,2,1,0:T(8,128)}, f32[3,3,128,256]{3,2,1,0:T(8,128)}, f32[3,3,256,512]{3,2,1,0:T(8,128)}), (f32[3,3,5,32,64]{4,3,2,1,0:T(8,128)}, f32[3,3,64,128]{3,2,1,0:T(8,128)}, ...) | async-done | bytes 6561808 | tf_op jit(solution)/shard_map/psum | solution.py:101
  385.6 2.1 copy.241
  387.7 1.7 copy.242
  390.4 5.0 %copy.244 = f32[3,3,256,512]{3,2,1,0:T(8,128)} copy(f32[3,3,256,512]{3,2,1,0:T(8,128)} %get-tuple-element.22) | data formatting | bytes 9437184
  (125 shorter events, 10.2 us)
Async XLA Ops:
  7.2 59.6 %copy-start = (bf16[3,3,256,512]{3,2,1,0:T(8,128)(2,1)S(1)}, bf16[3,3,256,512]{3,2,1,0:T(8,128)(2,1)}, u32[]{:S(2)}) copy-start(bf16[3,3,256,512]{3,2,1,0:T(8,128)(2,1)} %param.14) | copy-start | bytes 7077892
  7.2 378.4 %all-reduce.3.cloned.1.call-start = ((), (), s32[]{:S(2)}) async-start(), calls=%async_computation | async-start | bytes 13860864 | tf_op jit(solution)/shard_map/psum | solution.py:101
  12.7 7.8 %collective-permute-start = (bf16[1,160,1,128]{1,0,3,2:T(2,128)(2,1)S(1)}, bf16[1,160,1,128]{1,0,3,2:T(2,128)(2,1)S(1)}, u32[]{:S(2)}, u32[]{:S(2)}) collective-permute-start(bf16[1,160,1,128]{1,0,3,2:T(2,128)(2,1)S(1)} %slice.81), channel_id=1, source_target_pairs={{0,1},{1,2},{2,3},{3,4},{4,5},{5,6},{6,7},{8,9},{9,10},{10,11},{11... | collective-permute-start | bytes 122888 | tf_op jit(solution)/shard_map/ppermute | solution.py:10
  39.2 1.8 copy-start.15
  39.2 1.8 copy-start.17
  42.6 7.8 %copy-start.18 = (pred[8,5]{0,1:T(8,128)(4,1)S(1)}, pred[8,5]{0,1:T(8,128)(4,1)}, u32[]{:S(2)}) copy-start(pred[8,5]{0,1:T(8,128)(4,1)} %constant.40) | copy-start | bytes 124
  42.7 6.6 %collective-permute-start.1 = (bf16[1,64,1,64]{1,0,3,2:T(2,128)(2,1)S(1)}, bf16[1,64,1,64]{1,0,3,2:T(2,128)(2,1)S(1)}, u32[]{:S(2)}, u32[]{:S(2)}) collective-permute-start(bf16[1,64,1,64]{1,0,3,2:T(2,128)(2,1)S(1)} %slice_bitcast_fusion.1), channel_id=1, source_target_pairs={{0,1},{1,2},{2,3},{3,4},{4,5},{5,6},{6,7},{8,9},{9,10},{10,11},{11... | collective-permute-start | bytes 24584 | tf_op jit(solution)/shard_map/ppermute | solution.py:10
  49.8 9.5 %copy-start.3 = (bf16[1,64,9,64]{1,0,3,2:T(2,128)(2,1)}, bf16[1,64,9,64]{1,0,3,2:T(2,128)(2,1)S(1)}, u32[]{:S(2)}) copy-start(bf16[1,64,9,64]{1,0,3,2:T(2,128)(2,1)S(1)} %pad_maximum_fusion.1) | copy-start | bytes 221188
  49.8 9.3 %copy-start.19 = (pred[8,3]{0,1:T(4,128)(4,1)S(1)}, pred[8,3]{0,1:T(4,128)(4,1)}, u32[]{:S(2)}) copy-start(pred[8,3]{0,1:T(4,128)(4,1)} %constant.39) | copy-start | bytes 76
  50.2 14.4 %copy-start.10 = (bf16[512]{0:T(512)(128)(2,1)S(1)}, bf16[512]{0:T(512)(128)(2,1)}, u32[]{:S(2)}) copy-start(bf16[512]{0:T(512)(128)(2,1)} %param.15) | copy-start | bytes 3076
  50.3 8.8 %copy-start.5 = (bf16[3,3,128,256]{3,2,1,0:T(8,128)(2,1)S(1)}, bf16[3,3,128,256]{3,2,1,0:T(8,128)(2,1)}, u32[]{:S(2)}) copy-start(bf16[3,3,128,256]{3,2,1,0:T(8,128)(2,1)} %param.13) | copy-start | bytes 1769476
  52.3 14.4 %copy-start.14 = (pred[8,2]{0,1:T(4,128)(4,1)S(1)}, pred[8,2]{0,1:T(4,128)(4,1)}, u32[]{:S(2)}) copy-start(pred[8,2]{0,1:T(4,128)(4,1)} %constant.38) | copy-start | bytes 52
  52.4 6.0 %collective-permute-start.2 = (bf16[1,128,1,32]{1,0,3,2:T(2,128)(2,1)S(1)}, bf16[1,128,1,32]{1,0,3,2:T(2,128)(2,1)S(1)}, u32[]{:S(2)}, u32[]{:S(2)}) collective-permute-start(bf16[1,128,1,32]{1,0,3,2:T(2,128)(2,1)S(1)} %slice_bitcast_fusion.3), channel_id=1, source_target_pairs={{0,1},{1,2},{2,3},{3,4},{4,5},{5,6},{6,7},{8,9},{9,10},{10,11},{11... | collective-permute-start | bytes 24584 | tf_op jit(solution)/shard_map/ppermute | solution.py:10
  58.4 0.6 copy-start.8
  59.0 7.4 %copy-start.7 = (f32[4,8,5,128]{3,1,2,0:T(8,128)S(1)}, f32[4,8,5,128]{3,1,2,0:T(8,128)}, u32[]{:S(2)}) copy-start(f32[4,8,5,128]{3,1,2,0:T(8,128)} %get-tuple-element.11) | copy-start | bytes 245764
  59.4 7.1 %collective-permute-start.3 = (bf16[1,256,1,16]{1,0,3,2:T(2,128)(2,1)S(1)}, bf16[1,256,1,16]{1,0,3,2:T(2,128)(2,1)S(1)}, u32[]{:S(2)}, u32[]{:S(2)}) collective-permute-start(bf16[1,256,1,16]{1,0,3,2:T(2,128)(2,1)S(1)} %slice_bitcast_fusion.2), channel_id=1, source_target_pairs={{0,1},{1,2},{2,3},{3,4},{4,5},{5,6},{6,7},{8,9},{9,10},{10,11},{11... | collective-permute-start | bytes 24584 | tf_op jit(solution)/shard_map/ppermute | solution.py:10
  65.6 1.7 copy-start.16
  67.4 0.5 copy-start.12
  68.8 8.7 %copy-start.9 = (bf16[1,128,1,32]{1,0,3,2:T(2,128)(2,1)S(1)}, bf16[1,128,1,32]{1,0,3,2:T(2,128)(2,1)}, u32[]{:S(2)}) copy-start(bf16[1,128,1,32]{1,0,3,2:T(2,128)(2,1)} %copy-done.8) | copy-start | bytes 24580
  68.8 6.7 %collective-permute-start.4 = (f32[1,256,1,16]{1,0,3,2:T(1,128)S(1)}, f32[1,256,1,16]{1,0,3,2:T(1,128)S(1)}, u32[]{:S(2)}, u32[]{:S(2)}) collective-permute-start(f32[1,256,1,16]{1,0,3,2:T(1,128)S(1)} %get-tuple-element.14), channel_id=1, source_target_pairs={{1,0},{2,1},{3,2},{4,3},{5,4},{6,5},{7,6},{9,8},{10,9},{11,10},{12... | collective-permute-start | bytes 49160 | tf_op jit(solution)/shard_map/ppermute | solution.py:10
  76.0 7.3 %copy-start.6 = (bf16[3,3,64,128]{3,2,1,0:T(8,128)(2,1)S(1)}, bf16[3,3,64,128]{3,2,1,0:T(8,128)(2,1)}, u32[]{:S(2)}) copy-start(bf16[3,3,64,128]{3,2,1,0:T(8,128)(2,1)} %param.12) | copy-start | bytes 442372
  76.0 7.3 %copy-start.11 = (pred[8,10]{0,1:T(8,128)(4,1)S(1)}, pred[8,10]{0,1:T(8,128)(4,1)}, u32[]{:S(2)}) copy-start(pred[8,10]{0,1:T(8,128)(4,1)} %constant.37) | copy-start | bytes 244
  76.0 7.0 %collective-permute-start.5 = (f32[1,128,1,32]{1,0,3,2:T(1,128)S(1)}, f32[1,128,1,32]{1,0,3,2:T(1,128)S(1)}, u32[]{:S(2)}, u32[]{:S(2)}) collective-permute-start(f32[1,128,1,32]{1,0,3,2:T(1,128)S(1)} %slice.103), channel_id=1, source_target_pairs={{1,0},{2,1},{3,2},{4,3},{5,4},{6,5},{7,6},{9,8},{10,9},{11,10},{12... | collective-permute-start | bytes 49160 | tf_op jit(solution)/shard_map/ppermute | solution.py:10
  83.8 7.2 %copy-start.4 = (f32[8,1,64,64]{3,0,2,1:T(8,128)S(1)}, f32[8,1,64,64]{3,0,2,1:T(8,128)}, u32[]{:S(2)}) copy-start(f32[8,1,64,64]{3,0,2,1:T(8,128)} %slice.110) | copy-start | bytes 393220
  83.8 7.3 %copy-start.1 = (bf16[1,160,17,128]{1,0,3,2:T(2,128)(2,1)S(1)}, bf16[1,160,17,128]{1,0,3,2:T(2,128)(2,1)}, u32[]{:S(2)}) copy-start(bf16[1,160,17,128]{1,0,3,2:T(2,128)(2,1)} %pad_maximum_fusion) | copy-start | bytes 2088964
  83.8 7.2 %collective-permute-start.6 = (f32[1,64,1,64]{1,3,2,0:T(8,128)S(1)}, f32[1,64,1,64]{1,3,2,0:T(8,128)S(1)}, u32[]{:S(2)}, u32[]{:S(2)}) collective-permute-start(f32[1,64,1,64]{1,3,2,0:T(8,128)S(1)} %slice.109), channel_id=1, source_target_pairs={{1,0},{2,1},{3,2},{4,3},{5,4},{6,5},{7,6},{9,8},{10,9},{11,10},{12... | collective-permute-start | bytes 49160 | tf_op jit(solution)/shard_map/ppermute | solution.py:10
  96.7 0.7 copy-start.13
  385.6 3.8 copy-start.2
Sparse Core Ops, SparseCore 0:
  96.9 288.6 all-reduce.2
where the time goes:
time: 404 us; the launch traced here: 402 us
  waiting for transfers between devices  213 us (53%)
  blocking collectives  88.2 us (22%)
  local copies, waits for them, and re-layouts  33.2 us (8%)
  starting transfers between devices  25.9 us (6%)
  matrix products  20 us (5%)
  between operations  14.8 us (4%)
  other arithmetic  7.19 us (2%)
    psum x1, waiting for transfers between devices, local(): lax.psum((temporal_grad, middle_grad, deeper_grad, deepest_grad, head_gra...  200 us
    psum x1, blocking collectives, local(): lax.psum((temporal_grad, middle_grad, deeper_grad, deepest_grad, head_gra...  88.2 us
    ppermute x7, starting transfers between devices, from_behind(): return lax.ppermute(block, axis, route)  25.9 us
    unnamed x54, local copies, waits for them, and re-layouts  13.6 us
    ppermute x7, waiting for transfers between devices, from_behind(): return lax.ppermute(block, axis, route)  13.1 us
    conv_general_dilated x4, matrix products, weight_grad(): lax.conv_general_dilated(padded, delta, (1, 1), 'VALID', rhs_dilation=(2,...  12.7 us
  transfers between devices with their start and end apart: 8, of which 7 were waited for; matrix products, arithmetic and copies ran while one was open for 2% of the time, Pallas kernels for 0%

commit v1 on v0

v1 whole, which is shorter than its diff:
```python
import functools

import jax
import jax.numpy as jnp
from jax import lax
from jax.experimental import pallas as pl
from jax.experimental.pallas import tpu as pltpu
from jax.sharding import PartitionSpec as P

BF = jnp.bfloat16
F32 = jnp.float32
MESH = pl.DeviceIdType.MESH

NX, NY, NZ = 4, 4, 8
SIZE = {"x": NX, "y": NY, "z": NZ}
DEEPEST_AT, DEEPER_AT, TEMPORAL_AT, HEAD_AT, MIDDLE_AT = 0, 576, 720, 765, 768
PARTS = ((("x", "y", "z"), 12), (("y", "z", "x"), 4), (("z", "x", "y"), 3))
LENGTHS = tuple(SIZE[order[0]] * SIZE[order[1]] * kept for order, kept in PARTS)
STARTS = tuple(sum(LENGTHS[:i]) for i in range(len(PARTS)))
HALF = sum(LENGTHS)
TILES = 2 * HALF


def vmem():
    return pl.BlockSpec(memory_space=pltpu.VMEM)


def halo_kernel(occ_ref, window_ref, landed, send_sem, recv_sem):
    space = lax.axis_index("space")
    below = lax.rem(space + 1, 8)
    above = lax.rem(space + 7, 8)
    barrier = pltpu.get_barrier_semaphore()
    for peer in (below, above):
        pl.semaphore_signal(barrier, inc=1, device_id={"space": peer}, device_id_type=MESH)
    pl.semaphore_wait(barrier, 2)
    copy = pltpu.make_async_remote_copy(
        src_ref=occ_ref,
        dst_ref=landed,
        send_sem=send_sem,
        recv_sem=recv_sem,
        device_id={"space": below},
        device_id_type=MESH,
    )
    copy.start()
    window_ref[:, 16:32, :] = occ_ref[...]
    copy.wait()
    keep = jnp.where(space == 0, 0, 1)
    window_ref[:, 0:16, :] = landed[...] * keep


def halo(occ):
    return pl.pallas_call(
        halo_kernel,
        out_shape=jax.ShapeDtypeStruct((5, 32, 128), jnp.int32),
        in_specs=[vmem()],
        out_specs=vmem(),
        scratch_shapes=[
            pltpu.VMEM((5, 16, 128), jnp.int32),
            pltpu.SemaphoreType.DMA(()),
            pltpu.SemaphoreType.DMA(()),
        ],
        compiler_params=pltpu.CompilerParams(collective_id=0, has_side_effects=True),
    )(occ)


def dot(a, b):
    return lax.dot_general(a, b, (((1,), (0,)), ((), ())), preferred_element_type=F32)


def dot_nt(a, b):
    return lax.dot_general(a, b, (((1,), (1,)), ((), ())), preferred_element_type=F32)


def dot_tn(a, b):
    return lax.dot_general(a, b, (((0,), (0,)), ((), ())), preferred_element_type=F32)


def activate(pre):
    gate = jax.nn.sigmoid(pre)
    slope = gate * (1.0 + pre * (1.0 - gate))
    return pre * gate, slope


def later(block):
    rolled = pltpu.roll(block, 1, block.ndim - 2)
    index = lax.broadcasted_iota(jnp.int32, block.shape, block.ndim - 2)
    return jnp.where(index == 0, 0.0, rolled)


def sooner(block):
    size = block.shape[-2]
    rolled = pltpu.roll(block, size - 1, block.ndim - 2)
    index = lax.broadcasted_iota(jnp.int32, block.shape, block.ndim - 2)
    return jnp.where(index == size - 1, 0.0, rolled)


def tap_of(ref, p, q, rows, phases):
    a, b = p // 2, p % 2
    c, d = q // 2, q % 2
    block = ref[a : a + rows, b, c : c + phases, d]
    return block.reshape(rows * phases * block.shape[2], block.shape[3])


def store_map(ref, value, rows, phases):
    shifted = later(value[:, phases - 1])
    for r in range(rows):
        ref[r // 2, r % 2, 0, 0] = shifted[r].astype(BF)
        for m in range(phases):
            s = m + 1
            ref[r // 2, r % 2, s // 2, s % 2] = value[r, m].astype(BF)


def map_grad(delta, weight_ref, rows, phases):
    out = {}

    def put(r, m, value):
        out[(r, m)] = value if (r, m) not in out else out[(r, m)] + value

    for p in range(3):
        for q in range(3):
            part = dot_nt(delta, weight_ref[3 * p + q])
            part = part.reshape(rows, phases, 16, part.shape[1])
            for m in range(phases):
                s = 2 * m + q - 1
                for o in range(rows):
                    value = part[o, m]
                    if s < 0:
                        put(2 * o + p, 2 * phases - 1, sooner(value))
                    else:
                        put(2 * o + p, s, value)
    return out


def every_second(ref, r, start):
    halves = [ref[r, h, pl.ds(start, 16, stride=2), :] for h in range(2)]
    return jnp.concatenate(halves, axis=1)


def compute_kernel(
    window_ref,
    labels_ref,
    lift_ref,
    w1_ref,
    w2_ref,
    w3_ref,
    w4_ref,
    head_ref,
    grads_ref,
    lifted,
    first,
    first_slope,
    second,
    second_slope,
    third,
    third_slope,
    third_dx,
    first_delta,
):
    to = lax.broadcasted_iota(jnp.int32, (128, 128), 0)
    come = lax.broadcasted_iota(jnp.int32, (128, 128), 1)
    order = jnp.where(come == lax.rem(to, 16) * 8 + to // 16, 1.0, 0.0).astype(BF)
    shifts = lax.broadcasted_iota(jnp.int32, (16, 128), 0)
    lift = lift_ref[...]
    for r in range(31):
        frames = []
        for t in range(5):
            row = jnp.broadcast_to(window_ref[t, r + 1 : r + 2, :], (16, 128))
            bits = jnp.bitwise_and(jnp.right_shift(row, shifts), 1)
            frames.append(bits.astype(F32).astype(BF))
        turned = dot_nt(order, jnp.concatenate(frames, axis=0)).astype(BF)
        value = jnp.maximum(dot(turned, lift), 0.0).reshape(8, 16, 160)
        lifted[r // 2, r % 2, 0, 0] = later(value[7]).astype(BF)
        for m in range(8):
            s = m + 1
            lifted[r // 2, r % 2, s // 2, s % 2] = value[m].astype(BF)
    zero_row = jnp.zeros((5, 2, 16, 160), BF)
    lifted[15, 1] = zero_row
    lifted[16, 0] = zero_row
    lifted[16, 1] = zero_row

    pre = jnp.zeros((960, 64), F32)
    for p in range(3):
        for q in range(3):
            pre = pre + dot(tap_of(lifted, p, q, 15, 4), w1_ref[3 * p + q])
    value, slope = activate(pre)
    store_map(first, value.reshape(15, 4, 16, 64), 15, 4)
    first_slope[...] = slope.reshape(15, 4, 16, 64)

    pre = jnp.zeros((224, 128), F32)
    for p in range(3):
        for q in range(3):
            pre = pre + dot(tap_of(first, p, q, 7, 2), w2_ref[3 * p + q])
    value, slope = activate(pre)
    store_map(second, value.reshape(7, 2, 16, 128), 7, 2)
    second_slope[...] = slope.reshape(7, 2, 16, 128)

    pre = jnp.zeros((48, 256), F32)
    for p in range(3):
        for q in range(3):
            pre = pre + dot(tap_of(second, p, q, 3, 1), w3_ref[3 * p + q])
    value, slope = activate(pre)
    third[...] = jnp.zeros((3, 2, 32, 128), F32)
    for r in range(3):
        for h in range(2):
            third[r, h, 0:16, :] = value[16 * r : 16 * r + 16, 128 * h : 128 * h + 128]
    third_slope[...] = slope.reshape(3, 16, 256)

    place = lax.broadcasted_iota(jnp.int32, (16, 256), 0)
    cells = []
    pre = jnp.zeros((16, 512), F32)
    for p in range(3):
        even = every_second(third, p, 0)
        odd = every_second(third, p, 1)
        left = jnp.where((place > 0) & (place < 8), pltpu.roll(odd, 1, 0), 0.0)
        for q, block in enumerate((left, even, odd)):
            block = block.astype(BF)
            cells.append(block)
            pre = pre + dot(block, w4_ref[3 * p + q])
    value, slope = activate(pre)
    fourth = value.astype(BF).astype(F32)
    head = head_ref[...].astype(F32)
    logits = jnp.sum(fourth * head, axis=1, keepdims=True)
    logit_grad = (jax.nn.sigmoid(logits) - labels_ref[...].astype(F32)) / 32.0
    logit_grad = jnp.where(lax.broadcasted_iota(jnp.int32, (16, 1), 0) < 8, logit_grad, 0.0)
    head_grad = jnp.sum(fourth * logit_grad, axis=0, keepdims=True)
    grads_ref[HEAD_AT : HEAD_AT + 3] = jnp.zeros((3, 16, 128), BF)
    for lane in range(4):
        part = head_grad[:, 128 * lane : 128 * lane + 128]
        grads_ref[HEAD_AT, :, :] = jnp.where(
            lax.broadcasted_iota(jnp.int32, (16, 128), 0) == lane,
            jnp.broadcast_to(part, (16, 128)),
            grads_ref[HEAD_AT].astype(F32),
        ).astype(BF)
    grads_ref[804:TILES] = jnp.zeros((TILES - 804, 16, 128), BF)
    delta = (logit_grad * head * slope).astype(BF)

    for p in range(3):
        parts = []
        for q in range(3):
            t = 3 * p + q
            grad = dot_tn(cells[t], delta).astype(BF)
            for lane in range(4):
                grads_ref[64 * t + 16 * lane : 64 * t + 16 * lane + 16] = grad[
                    :, 128 * lane : 128 * lane + 128
                ].reshape(16, 16, 128)
            parts.append(dot_nt(delta, w4_ref[t]))
        odd = parts[2] + pltpu.roll(parts[0], 15, 0)
        for h in range(2):
            lanes = slice(128 * h, 128 * h + 128)
            third_dx[p, h, pl.ds(0, 16, stride=2), :] = parts[1][:, lanes]
            third_dx[p, h, pl.ds(1, 16, stride=2), :] = odd[:, lanes]
    delta = jnp.concatenate(
        [
            jnp.concatenate([third_dx[r, h, 0:16, :] for h in range(2)], axis=1) * third_slope[r]
            for r in range(3)
        ],
        axis=0,
    ).astype(BF)

    for t in range(9):
        grad = dot_tn(tap_of(second, t // 3, t % 3, 3, 1), delta).astype(BF)
        for lane in range(2):
            at = DEEPER_AT + 16 * t + 8 * lane
            grads_ref[at : at + 8] = grad[:, 128 * lane : 128 * lane + 128].reshape(8, 16, 128)
    dx = map_grad(delta, w3_ref, 3, 1)
    delta = jnp.concatenate(
        [dx[(r, m)] * second_slope[r, m] for r in range(7) for m in range(2)], axis=0
    ).astype(BF)

    for t in range(9):
        grad = dot_tn(tap_of(first, t // 3, t % 3, 7, 2), delta).astype(BF)
        at = MIDDLE_AT + 4 * t
        grads_ref[at : at + 4] = grad.reshape(4, 16, 128)
    dx = map_grad(delta, w2_ref, 7, 2)
    for r in range(15):
        for m in range(4):
            at = 64 * r + 16 * m
            first_delta[at : at + 16, :] = dx[(r, m)] * first_slope[r, m]
    first_delta[960:1024, :] = jnp.zeros((64, 64), F32)

    turned = jnp.transpose(first_delta[...]).astype(BF)
    for t in range(9):
        grad = dot(turned, tap_of(lifted, t // 3, t % 3, 16, 4))
        grad = jnp.transpose(grad)
        grad = jnp.concatenate([grad[0:80], grad[80:160]], axis=1).astype(BF)
        at = TEMPORAL_AT + 5 * t
        grads_ref[at : at + 5] = grad.reshape(5, 16, 128)


def compute(window, labels, lift, w1, w2, w3, w4, head):
    return pl.pallas_call(
        compute_kernel,
        out_shape=jax.ShapeDtypeStruct((TILES, 16, 128), BF),
        in_specs=[vmem()] * 8,
        out_specs=vmem(),
        scratch_shapes=[
            pltpu.VMEM((17, 2, 5, 2, 16, 160), BF),
            pltpu.VMEM((8, 2, 3, 2, 16, 64), BF),
            pltpu.VMEM((15, 4, 16, 64), F32),
            pltpu.VMEM((4, 2, 2, 2, 16, 128), BF),
            pltpu.VMEM((7, 2, 16, 128), F32),
            pltpu.VMEM((3, 2, 32, 128), F32),
            pltpu.VMEM((3, 16, 256), F32),
            pltpu.VMEM((3, 2, 32, 128), F32),
            pltpu.VMEM((1024, 64), F32),
        ],
        compiler_params=pltpu.CompilerParams(vmem_limit_bytes=48 * 1024 * 1024),
    )(window, labels, lift, w1, w2, w3, w4, head)


def position():
    dp = lax.axis_index("dp")
    space = lax.axis_index("space")
    return {
        "x": space // 2,
        "y": lax.rem(space, 2) * 2 + lax.rem(dp // 2, 2),
        "z": dp // 4,
        "core": lax.rem(dp, 2),
    }


def device_at(place):
    dp = place["z"] * 4 + lax.rem(place["y"], 2) * 2 + place["core"]
    space = place["x"] * 2 + place["y"] // 2
    return (dp, space)


def along(here, axis, distance):
    there = dict(here)
    there[axis] = lax.rem(here[axis] + distance, SIZE[axis])
    return there


def reduce_kernel(grads_ref, total_ref, *scratch):
    paired, *rest = scratch
    shared = rest[0:3]
    landed1, sum1 = rest[3:6], rest[6:9]
    landed2, sum2 = rest[9:12], rest[12:15]
    landed3 = rest[15:18]
    send_sem, recv_sem = rest[18], rest[19]

    here = position()
    core = here["core"]
    partner = dict(here)
    partner["core"] = 1 - core

    barrier = pltpu.get_barrier_semaphore()
    peers = [device_at(partner)]
    for axis, size in SIZE.items():
        peers += [device_at(along(here, axis, d)) for d in range(1, size)]
    for peer in peers:
        pl.semaphore_signal(barrier, inc=1, device_id=peer, device_id_type=MESH)
    pl.semaphore_wait(barrier, len(peers))

    used = [0]

    def send(src, dst, place):
        index = used[0]
        used[0] += 1
        copy = pltpu.make_async_remote_copy(
            src_ref=src,
            dst_ref=dst,
            send_sem=send_sem.at[index],
            recv_sem=recv_sem.at[index],
            device_id=device_at(place),
            device_id_type=MESH,
        )
        copy.start()
        return copy

    pending = []

    def arrive(copies):
        for copy in copies:
            copy.wait_recv()
        pending.extend(copies)

    flights = []
    for i in range(3):
        at = pl.ds((1 - core) * HALF + STARTS[i], LENGTHS[i])
        flights.append(
            [send(grads_ref.at[at], paired.at[pl.ds(STARTS[i], LENGTHS[i])], partner)]
        )

    for i, (order, kept) in enumerate(PARTS):
        first, second = SIZE[order[0]], SIZE[order[1]]
        arrive(flights[i])
        at = pl.ds(core * HALF + STARTS[i], LENGTHS[i])
        both = grads_ref[at].astype(F32) + paired[STARTS[i] : STARTS[i] + LENGTHS[i]].astype(F32)
        shared[i][...] = both.astype(BF).reshape(first, second * kept, 16, 128)
        flights[i] = []
        for d in range(1, first):
            there = along(here, order[0], d)
            flights[i].append(
                send(shared[i].at[there[order[0]]], landed1[i].at[d - 1], there)
            )

    for i, (order, kept) in enumerate(PARTS):
        first, second = SIZE[order[0]], SIZE[order[1]]
        arrive(flights[i])
        total = shared[i][here[order[0]]].astype(F32)
        for d in range(1, first):
            total = total + landed1[i][d - 1].astype(F32)
        sum1[i][...] = total.astype(BF).reshape(second, kept, 16, 128)
        flights[i] = []
        for d in range(1, second):
            there = along(here, order[1], d)
            flights[i].append(send(sum1[i].at[there[order[1]]], landed2[i].at[d - 1], there))

    for i, (order, kept) in enumerate(PARTS):
        second, third = SIZE[order[1]], SIZE[order[2]]
        arrive(flights[i])
        total = sum1[i][here[order[1]]].astype(F32)
        for d in range(1, second):
            total = total + landed2[i][d - 1].astype(F32)
        sum2[i][...] = total.astype(BF)
        flights[i] = []
        for d in range(1, third):
            there = along(here, order[2], d)
            flights[i].append(send(sum2[i], landed3[i].at[d - 1], there))

    for i, (order, kept) in enumerate(PARTS):
        second, third = SIZE[order[1]], SIZE[order[2]]
        mine = here[order[2]]
        arrive(flights[i])
        total = jnp.zeros((kept, 16, 128), F32)
        own = sum2[i][...].astype(F32)
        for k in range(third):
            back = lax.rem(mine - k + third, third)
            other = landed3[i][lax.rem(back + third - 1, third)].astype(F32)
            total = total + jnp.where(back == 0, own, other)
        at = core * HALF + STARTS[i] + here[order[0]] * (second * kept) + here[order[1]] * kept
        total_ref[pl.ds(at, kept)] = total.astype(BF)
        flights[i] = []
        for d in range(1, second):
            there = along(here, order[1], d)
            flights[i].append(
                send(total_ref.at[pl.ds(at, kept)], total_ref.at[pl.ds(at, kept)], there)
            )

    for i, (order, kept) in enumerate(PARTS):
        first, second = SIZE[order[0]], SIZE[order[1]]
        arrive(flights[i])
        at = core * HALF + STARTS[i] + here[order[0]] * (second * kept)
        flights[i] = []
        for d in range(1, first):
            there = along(here, order[0], d)
            flights[i].append(
                send(
                    total_ref.at[pl.ds(at, second * kept)],
                    total_ref.at[pl.ds(at, second * kept)],
                    there,
                )
            )

    for i in range(3):
        arrive(flights[i])
        at = pl.ds(core * HALF + STARTS[i], LENGTHS[i])
        flights[i] = [send(total_ref.at[at], total_ref.at[at], partner)]
    for i in range(3):
        arrive(flights[i])
    for copy in pending:
        copy.wait_send()


def all_reduce(grads):
    scratch = [pltpu.VMEM((HALF, 16, 128), BF)]
    dims = []
    for order, kept in PARTS:
        dims.append((SIZE[order[0]], SIZE[order[1]], SIZE[order[2]], kept))
    scratch += [pltpu.VMEM((a, b * k, 16, 128), BF) for a, b, c, k in dims]
    scratch += [pltpu.VMEM((a - 1, b * k, 16, 128), BF) for a, b, c, k in dims]
    scratch += [pltpu.VMEM((b, k, 16, 128), BF) for a, b, c, k in dims]
    scratch += [pltpu.VMEM((b - 1, k, 16, 128), BF) for a, b, c, k in dims]
    scratch += [pltpu.VMEM((k, 16, 128), BF) for a, b, c, k in dims]
    scratch += [pltpu.VMEM((c, k, 16, 128), BF) for a, b, c, k in dims]
    copies = 6 + sum(2 * (a - 1) + 2 * (b - 1) + (c - 1) for a, b, c, k in dims)
    scratch += [pltpu.SemaphoreType.DMA((copies,)), pltpu.SemaphoreType.DMA((copies,))]
    return pl.pallas_call(
        reduce_kernel,
        out_shape=jax.ShapeDtypeStruct((TILES, 16, 128), BF),
        in_specs=[vmem()],
        out_specs=vmem(),
        scratch_shapes=scratch,
        compiler_params=pltpu.CompilerParams(
            collective_id=1, has_side_effects=True, vmem_limit_bytes=48 * 1024 * 1024
        ),
    )(grads)


def unpack_kernel(d4, d3, d1, dh, d2, g1, g2, g3, g4, gh):
    for lane in range(4):
        g4[0, :, 128 * lane : 128 * lane + 128] = (
            d4[16 * lane : 16 * lane + 16].reshape(256, 128).astype(F32)
        )
    for lane in range(2):
        g3[0, :, 128 * lane : 128 * lane + 128] = (
            d3[8 * lane : 8 * lane + 8].reshape(128, 128).astype(F32)
        )
    g2[0] = d2[...].reshape(64, 128).astype(F32)
    block = d1[...].reshape(80, 128).astype(F32)
    g1[0, 0:80, :] = block[:, 0:64]
    g1[0, 80:160, :] = block[:, 64:128]
    gh[...] = dh[0, 0:8, :].astype(F32)


def unpack(total):
    return pl.pallas_call(
        unpack_kernel,
        grid=(9,),
        out_shape=[
            jax.ShapeDtypeStruct((9, 160, 64), F32),
            jax.ShapeDtypeStruct((9, 64, 128), F32),
            jax.ShapeDtypeStruct((9, 128, 256), F32),
            jax.ShapeDtypeStruct((9, 256, 512), F32),
            jax.ShapeDtypeStruct((8, 128), F32),
        ],
        in_specs=[
            pl.BlockSpec((64, 16, 128), lambda t: (t, 0, 0)),
            pl.BlockSpec((16, 16, 128), lambda t: (DEEPER_AT // 16 + t, 0, 0)),
            pl.BlockSpec((5, 16, 128), lambda t: (TEMPORAL_AT // 5 + t, 0, 0)),
            pl.BlockSpec((1, 16, 128), lambda t: (HEAD_AT, 0, 0)),
            pl.BlockSpec((4, 16, 128), lambda t: (MIDDLE_AT // 4 + t, 0, 0)),
        ],
        out_specs=[
            pl.BlockSpec((1, 160, 64), lambda t: (t, 0, 0)),
            pl.BlockSpec((1, 64, 128), lambda t: (t, 0, 0)),
            pl.BlockSpec((1, 128, 256), lambda t: (t, 0, 0)),
            pl.BlockSpec((1, 256, 512), lambda t: (t, 0, 0)),
            pl.BlockSpec((8, 128), lambda t: (0, 0)),
        ],
    )(total, total, total, total, total)


def local(
    occupancy,
    state_labels,
    lift_weight,
    temporal_weight,
    middle_weight,
    deeper_weight,
    deepest_weight,
    head_weight,
):
    window = halo(occupancy[0])
    labels = jnp.pad(state_labels.reshape(8, 1), ((0, 8), (0, 0)))
    padded = jnp.pad(lift_weight, ((0, 3), (0, 0)))
    spread = jnp.eye(5, dtype=BF)[:, None, :, None] * padded[None, :, None, :]
    grads = compute(
        window,
        labels,
        spread.reshape(80, 160),
        temporal_weight.reshape(9, 160, 64),
        middle_weight.reshape(9, 64, 128),
        deeper_weight.reshape(9, 128, 256),
        deepest_weight.reshape(9, 256, 512),
        head_weight.reshape(1, 512),
    )
    g1, g2, g3, g4, gh = unpack(all_reduce(grads))
    return (
        g1.reshape(3, 3, 5, 32, 64),
        g2.reshape(3, 3, 64, 128),
        g3.reshape(3, 3, 128, 256),
        g4.reshape(3, 3, 256, 512),
        gh[0:4].reshape(512),
    )


def solution(mesh):
    return jax.shard_map(
        local,
        mesh=mesh,
        in_specs=(
            P("dp", None, "space", None),
            P("dp", "space", None),
            P(),
            P(),
            P(),
            P(),
            P(),
            P(),
        ),
        out_specs=(P(), P(), P(), P(), P()),
        check_vma=False,
    )
```

time: 404 us -> 97.6 us (0.24)
  waiting for transfers between devices: 213 us -> 0 us
  blocking collectives: 88.2 us -> 0 us
  Pallas kernels: 0 us -> 85.5 us
  starting transfers between devices: 25.9 us -> 0 us
  local copies, waits for them, and re-layouts: 33.2 us -> 10.7 us
  matrix products: 20 us -> 0 us
  between operations: 14.8 us -> 0.68 us
  other arithmetic: 7.19 us -> 0.09 us
    psum x1 -> x0, waiting for transfers between devices: 200 us -> none  [local(): lax.psum((temporal_grad, middle_grad, deeper_grad, deepest_grad, head_gra...]
    psum x1 -> x0, blocking collectives: 88.2 us -> none  [local(): lax.psum((temporal_grad, middle_grad, deeper_grad, deepest_grad, head_gra...]
    pallas_call x0 -> x4, Pallas kernels: none -> 85.5 us  [the longest x1 58.1 us: all_reduce(): pl.pallas_call(reduce_kernel, out_shape=jax.ShapeDtypeStruct((TILES, 16,...]
    ppermute x7 -> x0, starting transfers between devices: 25.9 us -> none  [from_behind(): return lax.ppermute(block, axis, route)]
    conv_general_dilated x11 -> x0, matrix products: 18.4 us -> none  [the longest x4 12.7 us: weight_grad(): lax.conv_general_dilated(padded, delta, (1, 1), 'VALID', rhs_dilation=(2,...]
    ppermute x7 -> x0, waiting for transfers between devices: 13.1 us -> none  [from_behind(): return lax.ppermute(block, axis, route)]
    concatenate x6 -> x0, local copies, waits for them, and re-layouts: 7.66 us -> none  [conv_layer(): padded = jnp.concatenate([upper_row, feature_map], axis=2)]
    concatenate x4 -> x0, other arithmetic: 6.89 us -> none  [conv_layer(): padded = jnp.concatenate([upper_row, feature_map], axis=2)]
  transfers between devices with their start and end apart: 8 -> 0, of which waited for: 7 -> 0; matrix products, arithmetic and copies ran while one was open for 2% -> 0% of each run, Pallas kernels for 0% -> 0%
where the time goes in v1:
time: 97.6 us; the launch traced here: 97 us
  Pallas kernels  85.5 us (88%)
  local copies, waits for them, and re-layouts  10.7 us (11%)
    pallas_call x1, Pallas kernels, all_reduce(): pl.pallas_call(reduce_kernel, out_shape=jax.ShapeDtypeStruct((TILES, 16,...  58.1 us
    pallas_call x1, Pallas kernels, compute(): pl.pallas_call(compute_kernel, out_shape=jax.ShapeDtypeStruct((TILES, 16,...  11.6 us
    pallas_call x1, Pallas kernels, halo(): pl.pallas_call(halo_kernel, out_shape=jax.ShapeDtypeStruct((5, 32, 128),...  8.8 us
    unnamed x12, local copies, waits for them, and re-layouts  7.22 us
    pallas_call x1, Pallas kernels, unpack(): pl.pallas_call(unpack_kernel, grid=(9,), out_shape=[jax.ShapeDtypeStruct(...  7.01 us

profile of v1, /device:TPU:1, one launch (start us, length us, event | category | flops | bytes accessed | tf_op | source)
XLA Modules:
  0.0 97.0 jit_solution(11499712565815035735)
XLA Ops:
  0.6 0.7 reshape.61.head_ref
  1.3 0.7 copy.14
  2.1 0.7 pad.9
  2.8 8.8 %shard_map.119.window_ref = s32[5,32,128]{2,1,0:T(8,128)} custom-call(s32[5,16,128]{2,1,0:T(8,128)} %bitcast.16), custom_call_target="tpu_custom_call" | custom-call | tf_op jit(solution)/shard_map/pallas_call | solution.py:52
  11.6 0.1 broadcast_multiply_fusion
  11.6 0.1 mul.20.lift_ref
  11.8 0.0 copy-start.1
  11.8 1.7 %copy-done.1 = bf16[3,3,256,512]{3,2,1,0:T(8,128)(2,1)S(1)} copy-done((bf16[3,3,256,512]{3,2,1,0:T(8,128)(2,1)S(1)}, bf16[3,3,256,512]{3,2,1,0:T(8,128)(2,1)}, u32[]{:S(2)}) %copy-start.1) | copy-done | bytes 2359320
  13.4 0.0 copy-start.2
  13.4 1.1 %copy-done.2 = bf16[3,3,128,256]{3,2,1,0:T(8,128)(2,1)S(1)} copy-done((bf16[3,3,128,256]{3,2,1,0:T(8,128)(2,1)S(1)}, bf16[3,3,128,256]{3,2,1,0:T(8,128)(2,1)}, u32[]{:S(2)}) %copy-start.2) | copy-done | bytes 589848
  14.5 0.0 copy-start.3
  14.5 1.0 %copy-done.3 = bf16[3,3,5,32,64]{4,3,2,1,0:T(8,128)(2,1)S(1)} copy-done((bf16[3,3,5,32,64]{4,3,2,1,0:T(8,128)(2,1)S(1)}, bf16[3,3,5,32,64]{4,3,2,1,0:T(8,128)(2,1)}, u32[]{:S(2)}) %copy-start.3) | copy-done | bytes 184344
  15.5 0.0 copy-start.4
  15.5 0.9 copy-done.4
  16.4 0.0 copy-start.5
  16.4 0.9 copy-done.5
  17.3 11.6 %shard_map.120.grads_ref = bf16[832,16,128]{2,1,0:T(8,128)(2,1)} custom-call(s32[5,32,128]{2,1,0:T(8,128)S(1)} %copy-done.4, s32[16,1]{1,0:T(8,128)S(1)} %pad.8.labels_ref, bf16[80,160]{1,0:T(8,128)(2,1)S(1)} %mul.20.lift_ref, bf16[9,160,64]{2,1,0:T(8,128)(2,1)S(1)} %bitcast.14, bf16[9,64,128]{2,1,0:T(8,128)(2,1)S(1)} %bitcast.15, ...), custom_call_target="tpu_custom_call" | custom-call | tf_op jit(solution)/shard_map/pallas_call | solution.py:291
  28.9 58.1 %shard_map.121.d4.d3.d1.dh.d2 = bf16[832,16,128]{2,1,0:T(8,128)(2,1)S(1)} custom-call(bf16[832,16,128]{2,1,0:T(8,128)(2,1)} %shard_map.120.grads_ref), custom_call_target="tpu_custom_call" | custom-call | tf_op jit(solution)/shard_map/pallas_call | solution.py:479
  87.0 0.0 copy-start
  87.0 1.7 %copy-done = bf16[832,16,128]{2,1,0:T(8,128)(2,1)} copy-done((bf16[832,16,128]{2,1,0:T(8,128)(2,1)}, bf16[832,16,128]{2,1,0:T(8,128)(2,1)S(1)}, u32[]{:S(2)}) %copy-start) | copy-done | bytes 3407896
  88.7 7.0 %shard_map.122 = (f32[9,160,64]{2,1,0:T(8,128)}, f32[9,64,128]{2,1,0:T(8,128)}, f32[9,128,256]{2,1,0:T(8,128)}, f32[9,256,512]{2,1,0:T(8,128)}, f32[8,128]{1,0:T(8,128)}) custom-call(bf16[832,16,128]{2,1,0:T(8,128)(2,1)} %copy-done, bf16[832,16,128]{2,1,0:T(8,128)(2,1)} %copy-done, bf16[832,16,128]{2,1,0:T(8,128)(2,1)} %copy-done, ...), custom_call_target="tpu_custom_call" | custom-call | tf_op jit(solution)/shard_map/pallas_call | solution.py:508
  95.7 1.3 %slice_bitcast_fusion = f32[512]{0:T(512)} fusion(f32[8,128]{1,0:T(8,128)} %get-tuple-element.14), kind=kLoop, calls=%fused_computation.3 | loop fusion | bytes 4096 | tf_op jit(solution)/shard_map/reshape | solution.py:565
  (2 shorter events, 0.0 us)
Async XLA Ops:
  11.8 1.7 %copy-start.1 = (bf16[3,3,256,512]{3,2,1,0:T(8,128)(2,1)S(1)}, bf16[3,3,256,512]{3,2,1,0:T(8,128)(2,1)}, u32[]{:S(2)}) copy-start(bf16[3,3,256,512]{3,2,1,0:T(8,128)(2,1)} %param.14) | copy-start | bytes 7077892
  13.4 1.1 %copy-start.2 = (bf16[3,3,128,256]{3,2,1,0:T(8,128)(2,1)S(1)}, bf16[3,3,128,256]{3,2,1,0:T(8,128)(2,1)}, u32[]{:S(2)}) copy-start(bf16[3,3,128,256]{3,2,1,0:T(8,128)(2,1)} %param.13) | copy-start | bytes 1769476
  14.5 1.0 %copy-start.3 = (bf16[3,3,5,32,64]{4,3,2,1,0:T(8,128)(2,1)S(1)}, bf16[3,3,5,32,64]{4,3,2,1,0:T(8,128)(2,1)}, u32[]{:S(2)}) copy-start(bf16[3,3,5,32,64]{4,3,2,1,0:T(8,128)(2,1)} %param.11) | copy-start | bytes 552964
  15.5 0.9 copy-start.4
  16.4 0.9 copy-start.5
  87.0 1.7 %copy-start = (bf16[832,16,128]{2,1,0:T(8,128)(2,1)}, bf16[832,16,128]{2,1,0:T(8,128)(2,1)S(1)}, u32[]{:S(2)}) copy-start(bf16[832,16,128]{2,1,0:T(8,128)(2,1)S(1)} %shard_map.121.d4.d3.d1.dh.d2) | copy-start | bytes 10223620

commit v2 on v1

--- a/solution.py
+++ b/solution.py
@@ -1,4 +1,4 @@
-import functools
+import math
 
 import jax
 import jax.numpy as jnp
@@ -14,8 +14,18 @@
 NX, NY, NZ = 4, 4, 8
 SIZE = {"x": NX, "y": NY, "z": NZ}
 DEEPEST_AT, DEEPER_AT, TEMPORAL_AT, HEAD_AT, MIDDLE_AT = 0, 576, 720, 765, 768
-PARTS = ((("x", "y", "z"), 12), (("y", "z", "x"), 4), (("z", "x", "y"), 3))
-LENGTHS = tuple(SIZE[order[0]] * SIZE[order[1]] * kept for order, kept in PARTS)
+PARTS = (
+    (("z", "x", "y"), False, 5),
+    (("x", "y", "z"), True, 1),
+    (("y", "x", "z"), True, 1),
+)
+
+
+def shares(order, split):
+    return SIZE[order[0]], SIZE[order[1]], SIZE[order[2]] if split else 1
+
+
+LENGTHS = tuple(math.prod(shares(order, split)) * kept for order, split, kept in PARTS)
 STARTS = tuple(sum(LENGTHS[:i]) for i in range(len(PARTS)))
 HALF = sum(LENGTHS)
 TILES = 2 * HALF
@@ -327,23 +337,39 @@
 
 def along(here, axis, distance):
     there = dict(here)
-    there[axis] = lax.rem(here[axis] + distance, SIZE[axis])
+    size = SIZE[axis]
+    there[axis] = lax.rem(here[axis] + distance + size, size)
     return there
 
 
-def reduce_kernel(grads_ref, total_ref, *scratch):
-    paired, *rest = scratch
-    shared = rest[0:3]
-    landed1, sum1 = rest[3:6], rest[6:9]
-    landed2, sum2 = rest[9:12], rest[12:15]
-    landed3 = rest[15:18]
-    send_sem, recv_sem = rest[18], rest[19]
-
-    here = position()
-    core = here["core"]
+class Wires:
+    def __init__(self, send_sem, recv_sem):
+        self.send_sem, self.recv_sem = send_sem, recv_sem
+        self.used = 0
+        self.sent = []
+
+    def send(self, src, dst, place):
+        copy = pltpu.make_async_remote_copy(
+            src_ref=src,
+            dst_ref=dst,
+            send_sem=self.send_sem.at[self.used],
+            recv_sem=self.recv_sem.at[self.used],
+            device_id=device_at(place),
+            device_id_type=MESH,
+        )
+        self.used += 1
+        copy.start()
+        self.sent.append(copy)
+        return copy
+
+    def finish(self):
+        for copy in self.sent:
+            copy.wait_send()
+
+
+def greet(here):
     partner = dict(here)
-    partner["core"] = 1 - core
-
+    partner["core"] = 1 - here["core"]
     barrier = pltpu.get_barrier_semaphore()
     peers = [device_at(partner)]
     for axis, size in SIZE.items():
@@ -352,136 +378,240 @@
         pl.semaphore_signal(barrier, inc=1, device_id=peer, device_id_type=MESH)
     pl.semaphore_wait(barrier, len(peers))
 
-    used = [0]
-
-    def send(src, dst, place):
-        index = used[0]
-        used[0] += 1
-        copy = pltpu.make_async_remote_copy(
-            src_ref=src,
-            dst_ref=dst,
-            send_sem=send_sem.at[index],
-            recv_sem=recv_sem.at[index],
-            device_id=device_at(place),
-            device_id_type=MESH,
+
+def f32(block):
+    return block.astype(F32)
+
+
+def relayed_scatter(wires, here, axis, parts, right_in, left_in, right_out, left_out, m):
+    n = SIZE[axis]
+    half, h = n // 2, m // 2
+    me = here[axis]
+    right, left = along(here, axis, 1), along(here, axis, -1)
+
+    def chunk(distance):
+        return lax.rem(me + distance + n, n)
+
+    lo, hi = pl.ds(0, h), pl.ds(h, m - h)
+    far = chunk(half)
+    from_left = [wires.send(parts.at[far, lo], right_in.at[0, lo], right)]
+    from_right = [wires.send(parts.at[far, hi], left_in.at[0, hi], left)]
+    early_left = wires.send(parts.at[chunk(half - 1), hi], right_in.at[1, hi], right)
+    early_right = wires.send(parts.at[chunk(1 - half), lo], left_in.at[1, lo], left)
+    for s in range(1, half):
+        yield
+        to_right, to_left = chunk(half - s), chunk(s - half)
+        if s == 1:
+            from_left[-1].wait_recv()
+            right_out[0, 0:h] = (f32(parts[to_right, 0:h]) + f32(right_in[0, 0:h])).astype(BF)
+            from_left.append(wires.send(right_out.at[0, lo], right_in.at[1, lo], right))
+            from_right[-1].wait_recv()
+            left_out[0, h:m] = (f32(parts[to_left, h:m]) + f32(left_in[0, h:m])).astype(BF)
+            from_right.append(wires.send(left_out.at[0, hi], left_in.at[1, hi], left))
+        else:
+            if s == 2:
+                early_left.wait_recv()
+                early_right.wait_recv()
+            from_left[-1].wait_recv()
+            right_out[s - 1] = (f32(parts[to_right]) + f32(right_in[s - 1])).astype(BF)
+            from_left.append(wires.send(right_out.at[s - 1], right_in.at[s], right))
+            from_right[-1].wait_recv()
+            left_out[s - 1] = (f32(parts[to_left]) + f32(left_in[s - 1])).astype(BF)
+            from_right.append(wires.send(left_out.at[s - 1], left_in.at[s], left))
+    yield
+    if half == 2:
+        early_left.wait_recv()
+        early_right.wait_recv()
+    from_left[-1].wait_recv()
+    from_right[-1].wait_recv()
+    return f32(parts[me]) + f32(right_in[half - 1]) + f32(left_in[half - 1])
+
+
+def relayed_gather(wires, here, axis, total_ref, base, m, partner):
+    n = SIZE[axis]
+    half, h = n // 2, m // 2
+    me = here[axis]
+    right, left = along(here, axis, 1), along(here, axis, -1)
+    swapped = []
+
+    def piece(distance, at, size):
+        k = lax.rem(me + distance + n, n)
+        return total_ref.at[pl.ds(base + k * m + at, size)]
+
+    def swap(where):
+        swapped.append(wires.send(where, where, partner))
+
+    own = piece(0, 0, m)
+    from_left = wires.send(own, own, right)
+    from_right = wires.send(own, own, left)
+    swap(own)
+    for s in range(1, half):
+        yield
+        from_left.wait_recv()
+        at, size = (0, h) if s == half - 1 else (0, m)
+        here_now = piece(-s, at, size)
+        from_left = wires.send(here_now, here_now, right)
+        swap(piece(-s, 0, m))
+        from_right.wait_recv()
+        at, size = (h, m - h) if s == half - 1 else (0, m)
+        here_now = piece(s, at, size)
+        from_right = wires.send(here_now, here_now, left)
+        swap(piece(s, 0, m))
+    yield
+    from_left.wait_recv()
+    swap(piece(-half, 0, h))
+    from_right.wait_recv()
+    swap(piece(half, h, m - h))
+    yield
+    for copy in swapped:
+        copy.wait_recv()
+
+
+def direct_scatter(wires, here, axis, parts, landed):
+    n = SIZE[axis]
+    flights = []
+    for d in range(1, n):
+        there = along(here, axis, d)
+        flights.append(wires.send(parts.at[there[axis]], landed.at[d - 1], there))
+    yield
+    for copy in flights:
+        copy.wait_recv()
+    total = f32(parts[here[axis]])
+    for d in range(1, n):
+        total = total + f32(landed[d - 1])
+    return total
+
+
+def direct_gather(wires, here, axis, total_ref, base, m):
+    n = SIZE[axis]
+    own = total_ref.at[pl.ds(base + here[axis] * m, m)]
+    flights = [wires.send(own, own, along(here, axis, d)) for d in range(1, n)]
+    yield
+    for copy in flights:
+        copy.wait_recv()
+
+
+def direct_exchange(wires, here, axis, own, landed):
+    n = SIZE[axis]
+    me = here[axis]
+    flights = []
+    for d in range(1, n):
+        flights.append(wires.send(own, landed.at[d - 1], along(here, axis, d)))
+    yield
+    for copy in flights:
+        copy.wait_recv()
+    total = jnp.zeros(own.shape, F32)
+    for k in range(n):
+        back = lax.rem(me - k + n, n)
+        other = f32(landed[lax.rem(back + n - 1, n)])
+        total = total + jnp.where(back == 0, f32(own[...]), other)
+    return total
+
+
+def part_scratch(order, split, kept):
+    a, b, c = shares(order, split)
+    m = b * c * kept
+    return [
+        pltpu.VMEM((a, m, 16, 128), BF),
+        pltpu.VMEM((a // 2, m, 16, 128), BF),
+        pltpu.VMEM((a // 2, m, 16, 128), BF),
+        pltpu.VMEM((a // 2, m, 16, 128), BF),
+        pltpu.VMEM((a // 2, m, 16, 128), BF),
+        pltpu.VMEM((b, c * kept, 16, 128), BF),
+        pltpu.VMEM((b - 1, c * kept, 16, 128), BF),
+        pltpu.VMEM((c, kept, 16, 128), BF),
+        pltpu.VMEM((SIZE[order[2]], kept, 16, 128), BF),
+    ]
+
+
+def reduce_part(wires, here, partner, grads_ref, total_ref, paired, scratch, start, part):
+    shared, right_in, left_in, right_out, left_out, sum1, landed2, sum2, landed3 = scratch
+    order, split, kept = part
+    a, b, c = shares(order, split)
+    m = b * c * kept
+    core = here["core"]
+    there = pl.ds((1 - core) * HALF + start, a * m)
+    flight = wires.send(grads_ref.at[there], paired.at[pl.ds(start, a * m)], partner)
+    yield
+    flight.wait_recv()
+    both = f32(grads_ref[pl.ds(core * HALF + start, a * m)]) + f32(paired[start : start + a * m])
+    shared[...] = both.astype(BF).reshape(a, m, 16, 128)
+    total = yield from relayed_scatter(
+        wires, here, order[0], shared, right_in, left_in, right_out, left_out, m
+    )
+    sum1[...] = total.astype(BF).reshape(b, c * kept, 16, 128)
+    total = yield from direct_scatter(wires, here, order[1], sum1, landed2)
+    sum2[...] = total.astype(BF).reshape(c, kept, 16, 128)
+    if split:
+        total = yield from direct_scatter(wires, here, order[2], sum2, landed3)
+    else:
+        total = yield from direct_exchange(wires, here, order[2], sum2.at[0], landed3)
+    base0 = core * HALF + start
+    base1 = base0 + here[order[0]] * m
+    base2 = base1 + here[order[1]] * (c * kept)
+    if split:
+        total_ref[pl.ds(base2 + here[order[2]] * kept, kept)] = total.astype(BF)
+        yield from direct_gather(wires, here, order[2], total_ref, base2, kept)
+    else:
+        total_ref[pl.ds(base2, kept)] = total.astype(BF)
+    yield from direct_gather(wires, here, order[1], total_ref, base1, c * kept)
+    yield from relayed_gather(wires, here, order[0], total_ref, base0, m, partner)
+
+
+def interleave(programs):
+    programs = list(programs)
+    while programs:
+        still = []
+        for program in programs:
+            try:
+                next(program)
+                still.append(program)
+            except StopIteration:
+                pass
+        programs = still
+
+
+def reduce_all(here, grads_ref, total_ref, scratch):
+    paired, send_sem, recv_sem, *rest = scratch
+    partner = dict(here)
+    partner["core"] = 1 - here["core"]
+    wires = Wires(send_sem, recv_sem)
+    programs = []
+    for i, part in enumerate(PARTS):
+        scratch = rest[9 * i : 9 * i + 9]
+        programs.append(
+            reduce_part(
+                wires, here, partner, grads_ref, total_ref, paired, scratch, STARTS[i], part
+            )
         )
-        copy.start()
-        return copy
-
-    pending = []
-
-    def arrive(copies):
-        for copy in copies:
-            copy.wait_recv()
-        pending.extend(copies)
-
-    flights = []
-    for i in range(3):
-        at = pl.ds((1 - core) * HALF + STARTS[i], LENGTHS[i])
-        flights.append(
-            [send(grads_ref.at[at], paired.at[pl.ds(STARTS[i], LENGTHS[i])], partner)]
-        )
-
-    for i, (order, kept) in enumerate(PARTS):
-        first, second = SIZE[order[0]], SIZE[order[1]]
-        arrive(flights[i])
-        at = pl.ds(core * HALF + STARTS[i], LENGTHS[i])
-        both = grads_ref[at].astype(F32) + paired[STARTS[i] : STARTS[i] + LENGTHS[i]].astype(F32)
-        shared[i][...] = both.astype(BF).reshape(first, second * kept, 16, 128)
-        flights[i] = []
-        for d in range(1, first):
-            there = along(here, order[0], d)
-            flights[i].append(
-                send(shared[i].at[there[order[0]]], landed1[i].at[d - 1], there)
-            )
-
-    for i, (order, kept) in enumerate(PARTS):
-        first, second = SIZE[order[0]], SIZE[order[1]]
-        arrive(flights[i])
-        total = shared[i][here[order[0]]].astype(F32)
-        for d in range(1, first):
-            total = total + landed1[i][d - 1].astype(F32)
-        sum1[i][...] = total.astype(BF).reshape(second, kept, 16, 128)
-        flights[i] = []
-        for d in range(1, second):
-            there = along(here, order[1], d)
-            flights[i].append(send(sum1[i].at[there[order[1]]], landed2[i].at[d - 1], there))
-
-    for i, (order, kept) in enumerate(PARTS):
-        second, third = SIZE[order[1]], SIZE[order[2]]
-        arrive(flights[i])
-        total = sum1[i][here[order[1]]].astype(F32)
-        for d in range(1, second):
-            total = total + landed2[i][d - 1].astype(F32)
-        sum2[i][...] = total.astype(BF)
-        flights[i] = []
-        for d in range(1, third):
-            there = along(here, order[2], d)
-            flights[i].append(send(sum2[i], landed3[i].at[d - 1], there))
-
-    for i, (order, kept) in enumerate(PARTS):
-        second, third = SIZE[order[1]], SIZE[order[2]]
-        mine = here[order[2]]
-        arrive(flights[i])
-        total = jnp.zeros((kept, 16, 128), F32)
-        own = sum2[i][...].astype(F32)
-        for k in range(third):
-            back = lax.rem(mine - k + third, third)
-            other = landed3[i][lax.rem(back + third - 1, third)].astype(F32)
-            total = total + jnp.where(back == 0, own, other)
-        at = core * HALF + STARTS[i] + here[order[0]] * (second * kept) + here[order[1]] * kept
-        total_ref[pl.ds(at, kept)] = total.astype(BF)
-        flights[i] = []
-        for d in range(1, second):
-            there = along(here, order[1], d)
-            flights[i].append(
-                send(total_ref.at[pl.ds(at, kept)], total_ref.at[pl.ds(at, kept)], there)
-            )
-
-    for i, (order, kept) in enumerate(PARTS):
-        first, second = SIZE[order[0]], SIZE[order[1]]
-        arrive(flights[i])
-        at = core * HALF + STARTS[i] + here[order[0]] * (second * kept)
-        flights[i] = []
-        for d in range(1, first):
-            there = along(here, order[0], d)
-            flights[i].append(
-                send(
-                    total_ref.at[pl.ds(at, second * kept)],
-                    total_ref.at[pl.ds(at, second * kept)],
-                    there,
-                )
-            )
-
-    for i in range(3):
-        arrive(flights[i])
-        at = pl.ds(core * HALF + STARTS[i], LENGTHS[i])
-        flights[i] = [send(total_ref.at[at], total_ref.at[at], partner)]
-    for i in range(3):
-        arrive(flights[i])
-    for copy in pending:
-        copy.wait_send()
+    interleave(programs)
+    wires.finish()
+
+
+def reduce_scratch():
+    scratch = [
+        pltpu.VMEM((HALF, 16, 128), BF),
+        pltpu.SemaphoreType.DMA((128,)),
+        pltpu.SemaphoreType.DMA((128,)),
+    ]
+    for order, split, kept in PARTS:
+        scratch += part_scratch(order, split, kept)
+    return scratch
+
+
+def reduce_kernel(grads_ref, total_ref, *scratch):
+    here = position()
+    greet(here)
+    reduce_all(here, grads_ref, total_ref, scratch)
 
 
 def all_reduce(grads):
-    scratch = [pltpu.VMEM((HALF, 16, 128), BF)]
-    dims = []
-    for order, kept in PARTS:
-        dims.append((SIZE[order[0]], SIZE[order[1]], SIZE[order[2]], kept))
-    scratch += [pltpu.VMEM((a, b * k, 16, 128), BF) for a, b, c, k in dims]
-    scratch += [pltpu.VMEM((a - 1, b * k, 16, 128), BF) for a, b, c, k in dims]
-    scratch += [pltpu.VMEM((b, k, 16, 128), BF) for a, b, c, k in dims]
-    scratch += [pltpu.VMEM((b - 1, k, 16, 128), BF) for a, b, c, k in dims]
-    scratch += [pltpu.VMEM((k, 16, 128), BF) for a, b, c, k in dims]
-    scratch += [pltpu.VMEM((c, k, 16, 128), BF) for a, b, c, k in dims]
-    copies = 6 + sum(2 * (a - 1) + 2 * (b - 1) + (c - 1) for a, b, c, k in dims)
-    scratch += [pltpu.SemaphoreType.DMA((copies,)), pltpu.SemaphoreType.DMA((copies,))]
     return pl.pallas_call(
         reduce_kernel,
         out_shape=jax.ShapeDtypeStruct((TILES, 16, 128), BF),
         in_specs=[vmem()],
         out_specs=vmem(),
-        scratch_shapes=scratch,
+        scratch_shapes=reduce_scratch(),
         compiler_params=pltpu.CompilerParams(
             collective_id=1, has_side_effects=True, vmem_limit_bytes=48 * 1024 * 1024
         ),

time: 97.6 us -> 97.9 us (level)
  no operation moved by 1% of the time
where the time goes in v2:
time: 97.9 us; the launch traced here: 97.3 us
  Pallas kernels  85.8 us (88%)
  local copies, waits for them, and re-layouts  10.7 us (11%)
    pallas_call x1, Pallas kernels, all_reduce(): pl.pallas_call(reduce_kernel, out_shape=jax.ShapeDtypeStruct((TILES, 16,...  58.4 us
    pallas_call x1, Pallas kernels, compute(): pl.pallas_call(compute_kernel, out_shape=jax.ShapeDtypeStruct((TILES, 16,...  11.6 us
    pallas_call x1, Pallas kernels, halo(): pl.pallas_call(halo_kernel, out_shape=jax.ShapeDtypeStruct((5, 32, 128),...  8.8 us
    unnamed x12, local copies, waits for them, and re-layouts  7.22 us
    pallas_call x1, Pallas kernels, unpack(): pl.pallas_call(unpack_kernel, grid=(9,), out_shape=[jax.ShapeDtypeStruct(...  7.01 us

profile of v2, /device:TPU:1, one launch (start us, length us, event | category | flops | bytes accessed | tf_op | source)
XLA Modules:
  0.0 97.3 jit_solution(14399108874464225622)
XLA Ops:
  0.6 0.7 reshape.61.head_ref
  1.3 0.7 copy.14
  2.1 0.7 pad.9
  2.8 8.8 %shard_map.119.window_ref = s32[5,32,128]{2,1,0:T(8,128)} custom-call(s32[5,16,128]{2,1,0:T(8,128)} %bitcast.16), custom_call_target="tpu_custom_call" | custom-call | tf_op jit(solution)/shard_map/pallas_call | solution.py:62
  11.6 0.1 broadcast_multiply_fusion
  11.6 0.1 mul.20.lift_ref
  11.8 0.0 copy-start.1
  11.8 1.7 %copy-done.1 = bf16[3,3,256,512]{3,2,1,0:T(8,128)(2,1)S(1)} copy-done((bf16[3,3,256,512]{3,2,1,0:T(8,128)(2,1)S(1)}, bf16[3,3,256,512]{3,2,1,0:T(8,128)(2,1)}, u32[]{:S(2)}) %copy-start.1) | copy-done | bytes 2359320
  13.4 0.0 copy-start.2
  13.4 1.1 %copy-done.2 = bf16[3,3,128,256]{3,2,1,0:T(8,128)(2,1)S(1)} copy-done((bf16[3,3,128,256]{3,2,1,0:T(8,128)(2,1)S(1)}, bf16[3,3,128,256]{3,2,1,0:T(8,128)(2,1)}, u32[]{:S(2)}) %copy-start.2) | copy-done | bytes 589848
  14.5 0.0 copy-start.3
  14.5 1.0 %copy-done.3 = bf16[3,3,5,32,64]{4,3,2,1,0:T(8,128)(2,1)S(1)} copy-done((bf16[3,3,5,32,64]{4,3,2,1,0:T(8,128)(2,1)S(1)}, bf16[3,3,5,32,64]{4,3,2,1,0:T(8,128)(2,1)}, u32[]{:S(2)}) %copy-start.3) | copy-done | bytes 184344
  15.5 0.0 copy-start.4
  15.5 0.9 copy-done.4
  16.4 0.0 copy-start.5
  16.4 0.9 copy-done.5
  17.3 11.6 %shard_map.120.grads_ref = bf16[832,16,128]{2,1,0:T(8,128)(2,1)} custom-call(s32[5,32,128]{2,1,0:T(8,128)S(1)} %copy-done.4, s32[16,1]{1,0:T(8,128)S(1)} %pad.8.labels_ref, bf16[80,160]{1,0:T(8,128)(2,1)S(1)} %mul.20.lift_ref, bf16[9,160,64]{2,1,0:T(8,128)(2,1)S(1)} %bitcast.14, bf16[9,64,128]{2,1,0:T(8,128)(2,1)S(1)} %bitcast.15, ...), custom_call_target="tpu_custom_call" | custom-call | tf_op jit(solution)/shard_map/pallas_call | solution.py:301
  28.9 58.4 %shard_map.121.d4.d3.d1.dh.d2 = bf16[832,16,128]{2,1,0:T(8,128)(2,1)S(1)} custom-call(bf16[832,16,128]{2,1,0:T(8,128)(2,1)} %shard_map.120.grads_ref), custom_call_target="tpu_custom_call" | custom-call | tf_op jit(solution)/shard_map/pallas_call | solution.py:609
  87.3 0.0 copy-start
  87.3 1.7 %copy-done = bf16[832,16,128]{2,1,0:T(8,128)(2,1)} copy-done((bf16[832,16,128]{2,1,0:T(8,128)(2,1)}, bf16[832,16,128]{2,1,0:T(8,128)(2,1)S(1)}, u32[]{:S(2)}) %copy-start) | copy-done | bytes 3407896
  89.0 7.0 %shard_map.122 = (f32[9,160,64]{2,1,0:T(8,128)}, f32[9,64,128]{2,1,0:T(8,128)}, f32[9,128,256]{2,1,0:T(8,128)}, f32[9,256,512]{2,1,0:T(8,128)}, f32[8,128]{1,0:T(8,128)}) custom-call(bf16[832,16,128]{2,1,0:T(8,128)(2,1)} %copy-done, bf16[832,16,128]{2,1,0:T(8,128)(2,1)} %copy-done, bf16[832,16,128]{2,1,0:T(8,128)(2,1)} %copy-done, ...), custom_call_target="tpu_custom_call" | custom-call | tf_op jit(solution)/shard_map/pallas_call | solution.py:638
  96.0 1.3 %slice_bitcast_fusion = f32[512]{0:T(512)} fusion(f32[8,128]{1,0:T(8,128)} %get-tuple-element.14), kind=kLoop, calls=%fused_computation.3 | loop fusion | bytes 4096 | tf_op jit(solution)/shard_map/reshape | solution.py:695
  (2 shorter events, 0.0 us)
Async XLA Ops:
  11.8 1.7 %copy-start.1 = (bf16[3,3,256,512]{3,2,1,0:T(8,128)(2,1)S(1)}, bf16[3,3,256,512]{3,2,1,0:T(8,128)(2,1)}, u32[]{:S(2)}) copy-start(bf16[3,3,256,512]{3,2,1,0:T(8,128)(2,1)} %param.14) | copy-start | bytes 7077892
  13.4 1.1 %copy-start.2 = (bf16[3,3,128,256]{3,2,1,0:T(8,128)(2,1)S(1)}, bf16[3,3,128,256]{3,2,1,0:T(8,128)(2,1)}, u32[]{:S(2)}) copy-start(bf16[3,3,128,256]{3,2,1,0:T(8,128)(2,1)} %param.13) | copy-start | bytes 1769476
  14.5 1.0 %copy-start.3 = (bf16[3,3,5,32,64]{4,3,2,1,0:T(8,128)(2,1)S(1)}, bf16[3,3,5,32,64]{4,3,2,1,0:T(8,128)(2,1)}, u32[]{:S(2)}) copy-start(bf16[3,3,5,32,64]{4,3,2,1,0:T(8,128)(2,1)} %param.11) | copy-start | bytes 552964
  15.5 0.9 copy-start.4
  16.4 0.9 copy-start.5
  87.3 1.7 %copy-start = (bf16[832,16,128]{2,1,0:T(8,128)(2,1)}, bf16[832,16,128]{2,1,0:T(8,128)(2,1)S(1)}, u32[]{:S(2)}) copy-start(bf16[832,16,128]{2,1,0:T(8,128)(2,1)S(1)} %shard_map.121.d4.d3.d1.dh.d2) | copy-start | bytes 10223620

commit v3 on v2

--- a/solution.py
+++ b/solution.py
@@ -13,7 +13,8 @@
 
 NX, NY, NZ = 4, 4, 8
 SIZE = {"x": NX, "y": NY, "z": NZ}
-DEEPEST_AT, DEEPER_AT, TEMPORAL_AT, HEAD_AT, MIDDLE_AT = 0, 576, 720, 765, 768
+DEEPEST_AT, DEEPER_AT, MIDDLE_AT, TEMPORAL_AT = 0, 288, 360, 378
+HEAD_AT, HALF_ENDS = 398, (403, 399)
 PARTS = (
     (("z", "x", "y"), False, 5),
     (("x", "y", "z"), True, 1),
@@ -33,44 +34,6 @@
 
 def vmem():
     return pl.BlockSpec(memory_space=pltpu.VMEM)
-
-
-def halo_kernel(occ_ref, window_ref, landed, send_sem, recv_sem):
-    space = lax.axis_index("space")
-    below = lax.rem(space + 1, 8)
-    above = lax.rem(space + 7, 8)
-    barrier = pltpu.get_barrier_semaphore()
-    for peer in (below, above):
-        pl.semaphore_signal(barrier, inc=1, device_id={"space": peer}, device_id_type=MESH)
-    pl.semaphore_wait(barrier, 2)
-    copy = pltpu.make_async_remote_copy(
-        src_ref=occ_ref,
-        dst_ref=landed,
-        send_sem=send_sem,
-        recv_sem=recv_sem,
-        device_id={"space": below},
-        device_id_type=MESH,
-    )
-    copy.start()
-    window_ref[:, 16:32, :] = occ_ref[...]
-    copy.wait()
-    keep = jnp.where(space == 0, 0, 1)
-    window_ref[:, 0:16, :] = landed[...] * keep
-
-
-def halo(occ):
-    return pl.pallas_call(
-        halo_kernel,
-        out_shape=jax.ShapeDtypeStruct((5, 32, 128), jnp.int32),
-        in_specs=[vmem()],
-        out_specs=vmem(),
-        scratch_shapes=[
-            pltpu.VMEM((5, 16, 128), jnp.int32),
-            pltpu.SemaphoreType.DMA(()),
-            pltpu.SemaphoreType.DMA(()),
-        ],
-        compiler_params=pltpu.CompilerParams(collective_id=0, has_side_effects=True),
-    )(occ)
 
 
 def dot(a, b):
@@ -146,16 +109,41 @@
     return jnp.concatenate(halves, axis=1)
 
 
-def compute_kernel(
-    window_ref,
+def lift_row(order, shifts, lift, source, row, keep, lifted, r):
+    frames = []
+    for t in range(5):
+        line = source[t, row : row + 1, :]
+        if keep is not None:
+            line = line * keep
+        bits = jnp.bitwise_and(jnp.right_shift(jnp.broadcast_to(line, (16, 128)), shifts), 1)
+        frames.append(bits.astype(F32).astype(BF))
+    turned = dot_nt(order, jnp.concatenate(frames, axis=0)).astype(BF)
+    value = jnp.maximum(dot(turned, lift), 0.0).reshape(8, 16, 160)
+    lifted[r // 2, r % 2, 0, 0] = later(value[7]).astype(BF)
+    for m in range(8):
+        s = m + 1
+        lifted[r // 2, r % 2, s // 2, s % 2] = value[m].astype(BF)
+
+
+def step_kernel(
+    occ_ref,
     labels_ref,
     lift_ref,
+    w1_hbm,
+    w2_hbm,
+    w3_hbm,
+    w4_hbm,
+    head_ref,
+    total_ref,
     w1_ref,
     w2_ref,
     w3_ref,
     w4_ref,
-    head_ref,
+    weight_sem,
+    landed,
+    halo_sem,
     grads_ref,
+    lift_pad,
     lifted,
     first,
     first_slope,
@@ -165,29 +153,59 @@
     third_slope,
     third_dx,
     first_delta,
+    *reduce_scratch,
 ):
+    loads = [
+        pltpu.make_async_copy(source, target, weight_sem.at[i])
+        for i, (source, target) in enumerate(
+            ((w1_hbm, w1_ref), (w2_hbm, w2_ref), (w3_hbm, w3_ref), (w4_hbm, w4_ref))
+        )
+    ]
+    for load in loads:
+        load.start()
+    here = position()
+    space = lax.axis_index("space")
+    below = lax.rem(space + 1, 8)
+    above = lax.rem(space + 7, 8)
+    dp = lax.axis_index("dp")
+    greet(here, [(dp, below), (dp, above)])
+    halo = pltpu.make_async_remote_copy(
+        src_ref=occ_ref,
+        dst_ref=landed,
+        send_sem=halo_sem.at[0],
+        recv_sem=halo_sem.at[1],
+        device_id=(dp, below),
+        device_id_type=MESH,
+    )
+    halo.start()
+    reducing = Reduction(here, grads_ref, total_ref, reduce_scratch)
+
     to = lax.broadcasted_iota(jnp.int32, (128, 128), 0)
     come = lax.broadcasted_iota(jnp.int32, (128, 128), 1)
     order = jnp.where(come == lax.rem(to, 16) * 8 + to // 16, 1.0, 0.0).astype(BF)
     shifts = lax.broadcasted_iota(jnp.int32, (16, 128), 0)
-    lift = lift_ref[...]
-    for r in range(31):
-        frames = []
-        for t in range(5):
-            row = jnp.broadcast_to(window_ref[t, r + 1 : r + 2, :], (16, 128))
-            bits = jnp.bitwise_and(jnp.right_shift(row, shifts), 1)
-            frames.append(bits.astype(F32).astype(BF))
-        turned = dot_nt(order, jnp.concatenate(frames, axis=0)).astype(BF)
-        value = jnp.maximum(dot(turned, lift), 0.0).reshape(8, 16, 160)
-        lifted[r // 2, r % 2, 0, 0] = later(value[7]).astype(BF)
-        for m in range(8):
-            s = m + 1
-            lifted[r // 2, r % 2, s // 2, s % 2] = value[m].astype(BF)
+    lift_pad[...] = jnp.zeros((16, 32), F32)
+    lift_pad[0:13, :] = lift_ref[...].astype(F32)
+    wide = jnp.concatenate([lift_pad[...]] * 5, axis=1)
+    frame_of = lax.broadcasted_iota(jnp.int32, (16, 160), 1) // 32
+    lift = jnp.concatenate([jnp.where(frame_of == t, wide, 0.0) for t in range(5)], axis=0)
+    lift = lift.astype(BF)
     zero_row = jnp.zeros((5, 2, 16, 160), BF)
     lifted[15, 1] = zero_row
     lifted[16, 0] = zero_row
     lifted[16, 1] = zero_row
-
+    for half in range(2):
+        grads_ref[half * HALF + HALF_ENDS[half] : half * HALF + HALF] = jnp.zeros(
+            (HALF - HALF_ENDS[half], 16, 128), BF
+        )
+    for row in range(16):
+        lift_row(order, shifts, lift, occ_ref, row, None, lifted, row + 15)
+    halo.wait_recv()
+    keep = jnp.where(space == 0, 0, 1)
+    for row in range(1, 16):
+        lift_row(order, shifts, lift, landed, row, keep, lifted, row - 1)
+
+    loads[0].wait()
     pre = jnp.zeros((960, 64), F32)
     for p in range(3):
         for q in range(3):
@@ -196,6 +214,7 @@
     store_map(first, value.reshape(15, 4, 16, 64), 15, 4)
     first_slope[...] = slope.reshape(15, 4, 16, 64)
 
+    loads[1].wait()
     pre = jnp.zeros((224, 128), F32)
     for p in range(3):
         for q in range(3):
@@ -204,6 +223,7 @@
     store_map(second, value.reshape(7, 2, 16, 128), 7, 2)
     second_slope[...] = slope.reshape(7, 2, 16, 128)
 
+    loads[2].wait()
     pre = jnp.zeros((48, 256), F32)
     for p in range(3):
         for q in range(3):
@@ -215,6 +235,7 @@
             third[r, h, 0:16, :] = value[16 * r : 16 * r + 16, 128 * h : 128 * h + 128]
     third_slope[...] = slope.reshape(3, 16, 256)
 
+    loads[3].wait()
     place = lax.broadcasted_iota(jnp.int32, (16, 256), 0)
     cells = []
     pre = jnp.zeros((16, 512), F32)
@@ -228,32 +249,33 @@
             pre = pre + dot(block, w4_ref[3 * p + q])
     value, slope = activate(pre)
     fourth = value.astype(BF).astype(F32)
-    head = head_ref[...].astype(F32)
+    head = head_ref[...].astype(F32).reshape(1, 512)
     logits = jnp.sum(fourth * head, axis=1, keepdims=True)
-    logit_grad = (jax.nn.sigmoid(logits) - labels_ref[...].astype(F32)) / 32.0
+    cell = lax.broadcasted_iota(jnp.int32, (16, 8), 0)
+    lane = lax.broadcasted_iota(jnp.int32, (16, 8), 1)
+    labels = jnp.broadcast_to(labels_ref[...].astype(F32), (16, 8))
+    labels = jnp.sum(jnp.where(cell == lane, labels, 0.0), axis=1, keepdims=True)
+    logit_grad = (jax.nn.sigmoid(logits) - labels) / 32.0
     logit_grad = jnp.where(lax.broadcasted_iota(jnp.int32, (16, 1), 0) < 8, logit_grad, 0.0)
+    delta = (logit_grad * head * slope).astype(BF)
+
+    for t in range(9):
+        grad = dot_tn(cells[t], delta).astype(BF)
+        for lane in range(4):
+            at = (lane // 2) * HALF + DEEPEST_AT + 32 * t + 16 * (lane % 2)
+            grads_ref[at : at + 16] = grad[:, 128 * lane : 128 * lane + 128].reshape(16, 16, 128)
+        if t == 4:
+            reducing.begin(0)
+    reducing.begin(1)
     head_grad = jnp.sum(fourth * logit_grad, axis=0, keepdims=True)
-    grads_ref[HEAD_AT : HEAD_AT + 3] = jnp.zeros((3, 16, 128), BF)
+    row = lax.broadcasted_iota(jnp.int32, (16, 128), 0)
+    head_tile = jnp.zeros((16, 128), F32)
     for lane in range(4):
-        part = head_grad[:, 128 * lane : 128 * lane + 128]
-        grads_ref[HEAD_AT, :, :] = jnp.where(
-            lax.broadcasted_iota(jnp.int32, (16, 128), 0) == lane,
-            jnp.broadcast_to(part, (16, 128)),
-            grads_ref[HEAD_AT].astype(F32),
-        ).astype(BF)
-    grads_ref[804:TILES] = jnp.zeros((TILES - 804, 16, 128), BF)
-    delta = (logit_grad * head * slope).astype(BF)
-
+        part = jnp.broadcast_to(head_grad[:, 128 * lane : 128 * lane + 128], (16, 128))
+        head_tile = jnp.where(row == lane, part, head_tile)
+    grads_ref[HALF + HEAD_AT] = head_tile.astype(BF)
     for p in range(3):
-        parts = []
-        for q in range(3):
-            t = 3 * p + q
-            grad = dot_tn(cells[t], delta).astype(BF)
-            for lane in range(4):
-                grads_ref[64 * t + 16 * lane : 64 * t + 16 * lane + 16] = grad[
-                    :, 128 * lane : 128 * lane + 128
-                ].reshape(16, 16, 128)
-            parts.append(dot_nt(delta, w4_ref[t]))
+        parts = [dot_nt(delta, w4_ref[3 * p + q]) for q in range(3)]
         odd = parts[2] + pltpu.roll(parts[0], 15, 0)
         for h in range(2):
             lanes = slice(128 * h, 128 * h + 128)
@@ -269,41 +291,58 @@
 
     for t in range(9):
         grad = dot_tn(tap_of(second, t // 3, t % 3, 3, 1), delta).astype(BF)
-        for lane in range(2):
-            at = DEEPER_AT + 16 * t + 8 * lane
-            grads_ref[at : at + 8] = grad[:, 128 * lane : 128 * lane + 128].reshape(8, 16, 128)
+        for half in range(2):
+            at = half * HALF + DEEPER_AT + 8 * t
+            grads_ref[at : at + 8] = grad[:, 128 * half : 128 * half + 128].reshape(8, 16, 128)
     dx = map_grad(delta, w3_ref, 3, 1)
     delta = jnp.concatenate(
         [dx[(r, m)] * second_slope[r, m] for r in range(7) for m in range(2)], axis=0
     ).astype(BF)
+    reducing.advance(0)
 
     for t in range(9):
-        grad = dot_tn(tap_of(first, t // 3, t % 3, 7, 2), delta).astype(BF)
-        at = MIDDLE_AT + 4 * t
-        grads_ref[at : at + 4] = grad.reshape(4, 16, 128)
+        grad = dot_tn(tap_of(first, t // 3, t % 3, 7, 2), delta).astype(BF).reshape(4, 16, 128)
+        for half in range(2):
+            at = half * HALF + MIDDLE_AT + 2 * t
+            grads_ref[at : at + 2] = grad[2 * half : 2 * half + 2]
+    reducing.advance(1)
     dx = map_grad(delta, w2_ref, 7, 2)
     for r in range(15):
         for m in range(4):
             at = 64 * r + 16 * m
             first_delta[at : at + 16, :] = dx[(r, m)] * first_slope[r, m]
     first_delta[960:1024, :] = jnp.zeros((64, 64), F32)
+    reducing.advance(0)
 
     turned = jnp.transpose(first_delta[...]).astype(BF)
     for t in range(9):
         grad = dot(turned, tap_of(lifted, t // 3, t % 3, 16, 4))
         grad = jnp.transpose(grad)
         grad = jnp.concatenate([grad[0:80], grad[80:160]], axis=1).astype(BF)
-        at = TEMPORAL_AT + 5 * t
+        at = TEMPORAL_AT + 5 * t if t < 5 else HALF + TEMPORAL_AT + 5 * (t - 5)
         grads_ref[at : at + 5] = grad.reshape(5, 16, 128)
-
-
-def compute(window, labels, lift, w1, w2, w3, w4, head):
+    reducing.begin(2)
+    reducing.finish()
+    halo.wait_send()
+
+
+def step(occ, labels, lift, w1, w2, w3, w4, head):
+    hbm = pl.BlockSpec(memory_space=pl.ANY)
     return pl.pallas_call(
-        compute_kernel,
+        step_kernel,
         out_shape=jax.ShapeDtypeStruct((TILES, 16, 128), BF),
-        in_specs=[vmem()] * 8,
+        in_specs=[vmem()] * 3 + [hbm] * 4 + [vmem()],
         out_specs=vmem(),
         scratch_shapes=[
+            pltpu.VMEM(w1.shape, BF),
+            pltpu.VMEM(w2.shape, BF),
+            pltpu.VMEM(w3.shape, BF),
+            pltpu.VMEM(w4.shape, BF),
+            pltpu.SemaphoreType.DMA((4,)),
+            pltpu.VMEM((5, 16, 128), jnp.int32),
+            pltpu.SemaphoreType.DMA((2,)),
+            pltpu.VMEM((TILES, 16, 128), BF),
+            pltpu.VMEM((16, 32), F32),
             pltpu.VMEM((17, 2, 5, 2, 16, 160), BF),
             pltpu.VMEM((8, 2, 3, 2, 16, 64), BF),
             pltpu.VMEM((15, 4, 16, 64), F32),
@@ -313,9 +352,12 @@
             pltpu.VMEM((3, 16, 256), F32),
             pltpu.VMEM((3, 2, 32, 128), F32),
             pltpu.VMEM((1024, 64), F32),
-        ],
-        compiler_params=pltpu.CompilerParams(vmem_limit_bytes=48 * 1024 * 1024),
-    )(window, labels, lift, w1, w2, w3, w4, head)
+        ]
+        + reduce_scratch(),
+        compiler_params=pltpu.CompilerParams(
+            collective_id=0, has_side_effects=True, vmem_limit_bytes=50 * 1024 * 1024
+        ),
+    )(occ, labels, lift, w1, w2, w3, w4, head)
 
 
 def position():
@@ -367,11 +409,11 @@
             copy.wait_send()
 
 
-def greet(here):
+def greet(here, others):
     partner = dict(here)
     partner["core"] = 1 - here["core"]
     barrier = pltpu.get_barrier_semaphore()
-    peers = [device_at(partner)]
+    peers = [device_at(partner)] + others
     for axis, size in SIZE.items():
         peers += [device_at(along(here, axis, d)) for d in range(1, size)]
     for peer in peers:
@@ -571,21 +613,29 @@
         programs = still
 
 
-def reduce_all(here, grads_ref, total_ref, scratch):
-    paired, send_sem, recv_sem, *rest = scratch
-    partner = dict(here)
-    partner["core"] = 1 - here["core"]
-    wires = Wires(send_sem, recv_sem)
-    programs = []
-    for i, part in enumerate(PARTS):
-        scratch = rest[9 * i : 9 * i + 9]
-        programs.append(
-            reduce_part(
-                wires, here, partner, grads_ref, total_ref, paired, scratch, STARTS[i], part
+class Reduction:
+    def __init__(self, here, grads_ref, total_ref, scratch):
+        paired, send_sem, recv_sem, *rest = scratch
+        partner = dict(here)
+        partner["core"] = 1 - here["core"]
+        self.wires = Wires(send_sem, recv_sem)
+        self.programs = []
+        for i, part in enumerate(PARTS):
+            own = rest[9 * i : 9 * i + 9]
+            self.programs.append(
+                reduce_part(
+                    self.wires, here, partner, grads_ref, total_ref, paired, own, STARTS[i], part
+                )
             )
-        )
-    interleave(programs)
-    wires.finish()
+
+    def begin(self, i):
+        next(self.programs[i])
+
+    advance = begin
+
+    def finish(self):
+        interleave(self.programs)
+        self.wires.finish()
 
 
 def reduce_scratch():
@@ -599,67 +649,57 @@
     return scratch
 
 
-def reduce_kernel(grads_ref, total_ref, *scratch):
-    here = position()
-    greet(here)
-    reduce_all(here, grads_ref, total_ref, scratch)
-
-
-def all_reduce(grads):
-    return pl.pallas_call(
-        reduce_kernel,
-        out_shape=jax.ShapeDtypeStruct((TILES, 16, 128), BF),
-        in_specs=[vmem()],
-        out_specs=vmem(),
-        scratch_shapes=reduce_scratch(),
-        compiler_params=pltpu.CompilerParams(
-            collective_id=1, has_side_effects=True, vmem_limit_bytes=48 * 1024 * 1024
-        ),
-    )(grads)
-
-
-def unpack_kernel(d4, d3, d1, dh, d2, g1, g2, g3, g4, gh):
+def unpack_kernel(total_ref, g1, g2, g3, g4, gh, s1, s2, s3, s4, sem):
+    copies = []
+
+    def out(source, target):
+        copy = pltpu.make_async_copy(source, target, sem.at[len(copies)])
+        copy.start()
+        copies.append(copy)
+
+    for t in range(9):
+        for lane in range(4):
+            at = (lane // 2) * HALF + DEEPEST_AT + 32 * t + 16 * (lane % 2)
+            s4[t, :, 128 * lane : 128 * lane + 128] = f32(
+                total_ref[at : at + 16].reshape(256, 128)
+            )
+        out(s4.at[t], g4.at[t])
+    for t in range(9):
+        for half in range(2):
+            at = half * HALF + DEEPER_AT + 8 * t
+            s3[t, :, 128 * half : 128 * half + 128] = f32(
+                total_ref[at : at + 8].reshape(128, 128)
+            )
+    out(s3, g3)
+    for t in range(9):
+        for half in range(2):
+            at = half * HALF + MIDDLE_AT + 2 * t
+            s2[t, 32 * half : 32 * half + 32, :] = f32(total_ref[at : at + 2].reshape(32, 128))
+        at = TEMPORAL_AT + 5 * t if t < 5 else HALF + TEMPORAL_AT + 5 * (t - 5)
+        block = f32(total_ref[at : at + 5].reshape(80, 128))
+        s1[t, 0:80, :] = block[:, 0:64]
+        s1[t, 80:160, :] = block[:, 64:128]
+    out(s2, g2)
+    out(s1, g1)
+    tile = f32(total_ref[HALF + HEAD_AT])
     for lane in range(4):
-        g4[0, :, 128 * lane : 128 * lane + 128] = (
-            d4[16 * lane : 16 * lane + 16].reshape(256, 128).astype(F32)
-        )
-    for lane in range(2):
-        g3[0, :, 128 * lane : 128 * lane + 128] = (
-            d3[8 * lane : 8 * lane + 8].reshape(128, 128).astype(F32)
-        )
-    g2[0] = d2[...].reshape(64, 128).astype(F32)
-    block = d1[...].reshape(80, 128).astype(F32)
-    g1[0, 0:80, :] = block[:, 0:64]
-    g1[0, 80:160, :] = block[:, 64:128]
-    gh[...] = dh[0, 0:8, :].astype(F32)
+        gh[pl.ds(128 * lane, 128)] = tile[lane]
+    for copy in copies:
+        copy.wait()
 
 
 def unpack(total):
+    shapes = ((9, 160, 64), (9, 64, 128), (9, 128, 256), (9, 256, 512))
+    hbm = pl.BlockSpec(memory_space=pl.ANY)
     return pl.pallas_call(
         unpack_kernel,
-        grid=(9,),
-        out_shape=[
-            jax.ShapeDtypeStruct((9, 160, 64), F32),
-            jax.ShapeDtypeStruct((9, 64, 128), F32),
-            jax.ShapeDtypeStruct((9, 128, 256), F32),
-            jax.ShapeDtypeStruct((9, 256, 512), F32),
-            jax.ShapeDtypeStruct((8, 128), F32),
-        ],
-        in_specs=[
-            pl.BlockSpec((64, 16, 128), lambda t: (t, 0, 0)),
-            pl.BlockSpec((16, 16, 128), lambda t: (DEEPER_AT // 16 + t, 0, 0)),
-            pl.BlockSpec((5, 16, 128), lambda t: (TEMPORAL_AT // 5 + t, 0, 0)),
-            pl.BlockSpec((1, 16, 128), lambda t: (HEAD_AT, 0, 0)),
-            pl.BlockSpec((4, 16, 128), lambda t: (MIDDLE_AT // 4 + t, 0, 0)),
-        ],
-        out_specs=[
-            pl.BlockSpec((1, 160, 64), lambda t: (t, 0, 0)),
-            pl.BlockSpec((1, 64, 128), lambda t: (t, 0, 0)),
-            pl.BlockSpec((1, 128, 256), lambda t: (t, 0, 0)),
-            pl.BlockSpec((1, 256, 512), lambda t: (t, 0, 0)),
-            pl.BlockSpec((8, 128), lambda t: (0, 0)),
-        ],
-    )(total, total, total, total, total)
+        out_shape=[jax.ShapeDtypeStruct(shape, F32) for shape in shapes + ((512,),)],
+        in_specs=[vmem()],
+        out_specs=[hbm] * 4 + [vmem()],
+        scratch_shapes=[pltpu.VMEM(shape, F32) for shape in shapes]
+        + [pltpu.SemaphoreType.DMA((12,))],
+        compiler_params=pltpu.CompilerParams(vmem_limit_bytes=40 * 1024 * 1024),
+    )(total)
 
 
 def local(
@@ -672,27 +712,23 @@
     deepest_weight,
     head_weight,
 ):
-    window = halo(occupancy[0])
-    labels = jnp.pad(state_labels.reshape(8, 1), ((0, 8), (0, 0)))
-    padded = jnp.pad(lift_weight, ((0, 3), (0, 0)))
-    spread = jnp.eye(5, dtype=BF)[:, None, :, None] * padded[None, :, None, :]
-    grads = compute(
-        window,
-        labels,
-        spread.reshape(80, 160),
+    total = step(
+        occupancy[0],
+        state_labels[0],
+        lift_weight,
         temporal_weight.reshape(9, 160, 64),
         middle_weight.reshape(9, 64, 128),
         deeper_weight.reshape(9, 128, 256),
         deepest_weight.reshape(9, 256, 512),
-        head_weight.reshape(1, 512),
+        head_weight,
     )
-    g1, g2, g3, g4, gh = unpack(all_reduce(grads))
+    g1, g2, g3, g4, gh = unpack(total)
     return (
         g1.reshape(3, 3, 5, 32, 64),
         g2.reshape(3, 3, 64, 128),
         g3.reshape(3, 3, 128, 256),
         g4.reshape(3, 3, 256, 512),
-        gh[0:4].reshape(512),
+        gh,
     )
 
 

time: 97.9 us -> 85.8 us (0.88)
  Pallas kernels: 85.8 us -> 75.4 us
  local copies, waits for them, and re-layouts: 10.7 us -> 9.37 us
    pallas_call x4 -> x2, Pallas kernels: 85.8 us -> 75.4 us  [the longest x1 71.8 us: step(): pl.pallas_call(step_kernel, out_shape=jax.ShapeDtypeStruct((TILES, 16, 12...]
    reshape x3 -> x0, local copies, waits for them, and re-layouts: 2.67 us -> none  [the longest x1 1.26 us: local(): gh[0:4].reshape(512)]
    unnamed x12 -> x18, local copies, waits for them, and re-layouts: 7.22 us -> 9.37 us
where the time goes in v3:
time: 85.8 us; the launch traced here: 85.4 us
  Pallas kernels  75.4 us (88%)
  local copies, waits for them, and re-layouts  9.37 us (11%)
    pallas_call x1, Pallas kernels, step(): pl.pallas_call(step_kernel, out_shape=jax.ShapeDtypeStruct((TILES, 16, 12...  71.8 us
    unnamed x18, local copies, waits for them, and re-layouts  9.37 us
    pallas_call x1, Pallas kernels, unpack(): pl.pallas_call(unpack_kernel, out_shape=[jax.ShapeDtypeStruct(shape, F32)...  3.6 us

profile of v3, /device:TPU:1, one launch (start us, length us, event | category | flops | bytes accessed | tf_op | source)
XLA Modules:
  0.0 85.4 jit_solution(15891343430793416472)
XLA Ops:
  0.6 0.0 copy-start.1
  0.6 1.7 %copy-done.1 = bf16[3,3,256,512]{3,2,1,0:T(8,128)(2,1)S(1)} copy-done((bf16[3,3,256,512]{3,2,1,0:T(8,128)(2,1)S(1)}, bf16[3,3,256,512]{3,2,1,0:T(8,128)(2,1)}, u32[]{:S(2)}) %copy-start.1) | copy-done | bytes 2359320
  2.3 0.0 copy-start.2
  2.3 1.1 %copy-done.2 = bf16[3,3,128,256]{3,2,1,0:T(8,128)(2,1)S(1)} copy-done((bf16[3,3,128,256]{3,2,1,0:T(8,128)(2,1)S(1)}, bf16[3,3,128,256]{3,2,1,0:T(8,128)(2,1)}, u32[]{:S(2)}) %copy-start.2) | copy-done | bytes 589848
  3.4 0.0 copy-start.3
  3.4 1.0 %copy-done.3 = bf16[3,3,5,32,64]{4,3,2,1,0:T(8,128)(2,1)S(1)} copy-done((bf16[3,3,5,32,64]{4,3,2,1,0:T(8,128)(2,1)S(1)}, bf16[3,3,5,32,64]{4,3,2,1,0:T(8,128)(2,1)}, u32[]{:S(2)}) %copy-start.3) | copy-done | bytes 184344
  4.4 0.0 copy-start.4
  4.4 0.9 %copy-done.4 = bf16[3,3,64,128]{3,2,1,0:T(8,128)(2,1)S(1)} copy-done((bf16[3,3,64,128]{3,2,1,0:T(8,128)(2,1)S(1)}, bf16[3,3,64,128]{3,2,1,0:T(8,128)(2,1)}, u32[]{:S(2)}) %copy-start.4) | copy-done | bytes 147480
  5.3 0.0 copy-start.5
  5.3 0.8 copy-done.5
  6.0 0.0 copy-start.6
  6.0 0.7 copy-done.6
  6.7 0.0 copy-start.7
  6.7 0.7 copy-done.7
  7.4 0.0 copy-start.8
  7.4 0.7 copy-done.8
  8.1 71.8 %shard_map.119.total_ref = bf16[832,16,128]{2,1,0:T(8,128)(2,1)} custom-call(s32[5,16,128]{2,1,0:T(8,128)S(1)} %bitcast.14, s32[1,8]{1,0:T(1,128)S(1)} %bitcast.15, bf16[13,32]{1,0:T(8,128)(2,1)S(1)} %copy-done.6, bf16[9,160,64]{2,1,0:T(8,128)(2,1)S(1)} %bitcast.12, bf16[9,64,128]{2,1,0:T(8,128)(2,1)S(1)} %bitcast.13, bf16[9,128,256]{2,1,0:T(8,128)(2,1)S(1)} %bitcast.11, ...), custom_call_target="tpu_custom_call" | custom-call | tf_op jit(solution)/shard_map/pallas_call | solution.py:331
  79.8 0.0 copy-start
  79.8 2.0 %copy-done = bf16[832,16,128]{2,1,0:T(8,128)(2,1)S(1)} copy-done((bf16[832,16,128]{2,1,0:T(8,128)(2,1)S(1)}, bf16[832,16,128]{2,1,0:T(8,128)(2,1)}, u32[]{:S(2)}) %copy-start) | copy-done | bytes 3407896
  81.8 3.6 %shard_map.120 = (f32[9,160,64]{2,1,0:T(8,128)}, f32[9,64,128]{2,1,0:T(8,128)}, f32[9,128,256]{2,1,0:T(8,128)}, f32[9,256,512]{2,1,0:T(8,128)}, f32[512]{0:T(512)}) custom-call(bf16[832,16,128]{2,1,0:T(8,128)(2,1)S(1)} %copy-done), custom_call_target="tpu_custom_call" | custom-call | tf_op jit(solution)/shard_map/pallas_call | solution.py:694
Async XLA Ops:
  0.6 1.7 %copy-start.1 = (bf16[3,3,256,512]{3,2,1,0:T(8,128)(2,1)S(1)}, bf16[3,3,256,512]{3,2,1,0:T(8,128)(2,1)}, u32[]{:S(2)}) copy-start(bf16[3,3,256,512]{3,2,1,0:T(8,128)(2,1)} %param.14) | copy-start | bytes 7077892
  2.3 1.1 %copy-start.2 = (bf16[3,3,128,256]{3,2,1,0:T(8,128)(2,1)S(1)}, bf16[3,3,128,256]{3,2,1,0:T(8,128)(2,1)}, u32[]{:S(2)}) copy-start(bf16[3,3,128,256]{3,2,1,0:T(8,128)(2,1)} %param.13) | copy-start | bytes 1769476
  3.4 1.0 %copy-start.3 = (bf16[3,3,5,32,64]{4,3,2,1,0:T(8,128)(2,1)S(1)}, bf16[3,3,5,32,64]{4,3,2,1,0:T(8,128)(2,1)}, u32[]{:S(2)}) copy-start(bf16[3,3,5,32,64]{4,3,2,1,0:T(8,128)(2,1)} %param.11) | copy-start | bytes 552964
  4.4 0.9 %copy-start.4 = (bf16[3,3,64,128]{3,2,1,0:T(8,128)(2,1)S(1)}, bf16[3,3,64,128]{3,2,1,0:T(8,128)(2,1)}, u32[]{:S(2)}) copy-start(bf16[3,3,64,128]{3,2,1,0:T(8,128)(2,1)} %param.12) | copy-start | bytes 442372
  5.3 0.8 copy-start.5
  6.0 0.7 copy-start.6
  6.7 0.7 copy-start.7
  7.4 0.7 copy-start.8
  79.8 2.0 %copy-start = (bf16[832,16,128]{2,1,0:T(8,128)(2,1)S(1)}, bf16[832,16,128]{2,1,0:T(8,128)(2,1)}, u32[]{:S(2)}) copy-start(bf16[832,16,128]{2,1,0:T(8,128)(2,1)} %shard_map.119.total_ref) | copy-start | bytes 10223620

commit v4 on v3

--- a/solution.py
+++ b/solution.py
@@ -16,9 +16,11 @@
 DEEPEST_AT, DEEPER_AT, MIDDLE_AT, TEMPORAL_AT = 0, 288, 360, 378
 HEAD_AT, HALF_ENDS = 398, (403, 399)
 PARTS = (
-    (("z", "x", "y"), False, 5),
+    (("z", "x", "y"), False, 3),
     (("x", "y", "z"), True, 1),
     (("y", "x", "z"), True, 1),
+    (("x", "y", "z"), False, 2),
+    (("y", "x", "z"), False, 2),
 )
 
 
@@ -264,9 +266,10 @@
         for lane in range(4):
             at = (lane // 2) * HALF + DEEPEST_AT + 32 * t + 16 * (lane % 2)
             grads_ref[at : at + 16] = grad[:, 128 * lane : 128 * lane + 128].reshape(16, 16, 128)
-        if t == 4:
+        if t == 2:
             reducing.begin(0)
-    reducing.begin(1)
+        if t == 6:
+            reducing.begin(1)
     head_grad = jnp.sum(fourth * logit_grad, axis=0, keepdims=True)
     row = lax.broadcasted_iota(jnp.int32, (16, 128), 0)
     head_tile = jnp.zeros((16, 128), F32)
@@ -289,11 +292,15 @@
         axis=0,
     ).astype(BF)
 
+    reducing.advance(0)
+
     for t in range(9):
         grad = dot_tn(tap_of(second, t // 3, t % 3, 3, 1), delta).astype(BF)
         for half in range(2):
             at = half * HALF + DEEPER_AT + 8 * t
             grads_ref[at : at + 8] = grad[:, 128 * half : 128 * half + 128].reshape(8, 16, 128)
+    reducing.begin(2)
+    reducing.advance(1)
     dx = map_grad(delta, w3_ref, 3, 1)
     delta = jnp.concatenate(
         [dx[(r, m)] * second_slope[r, m] for r in range(7) for m in range(2)], axis=0
@@ -305,7 +312,7 @@
         for half in range(2):
             at = half * HALF + MIDDLE_AT + 2 * t
             grads_ref[at : at + 2] = grad[2 * half : 2 * half + 2]
-    reducing.advance(1)
+    reducing.advance(2)
     dx = map_grad(delta, w2_ref, 7, 2)
     for r in range(15):
         for m in range(4):
@@ -313,6 +320,7 @@
             first_delta[at : at + 16, :] = dx[(r, m)] * first_slope[r, m]
     first_delta[960:1024, :] = jnp.zeros((64, 64), F32)
     reducing.advance(0)
+    reducing.advance(1)
 
     turned = jnp.transpose(first_delta[...]).astype(BF)
     for t in range(9):
@@ -321,7 +329,11 @@
         grad = jnp.concatenate([grad[0:80], grad[80:160]], axis=1).astype(BF)
         at = TEMPORAL_AT + 5 * t if t < 5 else HALF + TEMPORAL_AT + 5 * (t - 5)
         grads_ref[at : at + 5] = grad.reshape(5, 16, 128)
-    reducing.begin(2)
+        if t == 4:
+            reducing.advance(0)
+            reducing.advance(2)
+    reducing.begin(3)
+    reducing.begin(4)
     reducing.finish()
     halo.wait_send()
 
@@ -355,7 +367,7 @@
         ]
         + reduce_scratch(),
         compiler_params=pltpu.CompilerParams(
-            collective_id=0, has_side_effects=True, vmem_limit_bytes=50 * 1024 * 1024
+            collective_id=0, has_side_effects=True, vmem_limit_bytes=67043328
         ),
     )(occ, labels, lift, w1, w2, w3, w4, head)
 
@@ -641,15 +653,25 @@
 def reduce_scratch():
     scratch = [
         pltpu.VMEM((HALF, 16, 128), BF),
-        pltpu.SemaphoreType.DMA((128,)),
-        pltpu.SemaphoreType.DMA((128,)),
+        pltpu.SemaphoreType.DMA((192,)),
+        pltpu.SemaphoreType.DMA((192,)),
     ]
     for order, split, kept in PARTS:
         scratch += part_scratch(order, split, kept)
     return scratch
 
 
-def unpack_kernel(total_ref, g1, g2, g3, g4, gh, s1, s2, s3, s4, sem):
+def unpack_kernel(total_hbm, g1, g2, g3, g4, gh, total_ref, s1, s2, s3, s4, load_sem, sem):
+    spans = [(32 * t, 32) for t in range(9)] + [(DEEPER_AT, HALF - DEEPER_AT)]
+    loads = []
+    for i, (at, size) in enumerate(spans):
+        for half in range(2):
+            where = pl.ds(half * HALF + at, size)
+            load = pltpu.make_async_copy(
+                total_hbm.at[where], total_ref.at[where], load_sem.at[2 * i + half]
+            )
+            load.start()
+            loads.append(load)
     copies = []
 
     def out(source, target):
@@ -658,12 +680,16 @@
         copies.append(copy)
 
     for t in range(9):
+        loads[2 * t].wait()
+        loads[2 * t + 1].wait()
         for lane in range(4):
             at = (lane // 2) * HALF + DEEPEST_AT + 32 * t + 16 * (lane % 2)
             s4[t, :, 128 * lane : 128 * lane + 128] = f32(
                 total_ref[at : at + 16].reshape(256, 128)
             )
         out(s4.at[t], g4.at[t])
+    loads[18].wait()
+    loads[19].wait()
     for t in range(9):
         for half in range(2):
             at = half * HALF + DEEPER_AT + 8 * t
@@ -694,11 +720,12 @@
     return pl.pallas_call(
         unpack_kernel,
         out_shape=[jax.ShapeDtypeStruct(shape, F32) for shape in shapes + ((512,),)],
-        in_specs=[vmem()],
+        in_specs=[hbm],
         out_specs=[hbm] * 4 + [vmem()],
-        scratch_shapes=[pltpu.VMEM(shape, F32) for shape in shapes]
-        + [pltpu.SemaphoreType.DMA((12,))],
-        compiler_params=pltpu.CompilerParams(vmem_limit_bytes=40 * 1024 * 1024),
+        scratch_shapes=[pltpu.VMEM((TILES, 16, 128), BF)]
+        + [pltpu.VMEM(shape, F32) for shape in shapes]
+        + [pltpu.SemaphoreType.DMA((20,)), pltpu.SemaphoreType.DMA((12,))],
+        compiler_params=pltpu.CompilerParams(vmem_limit_bytes=67043328),
     )(total)
 
 

time: 85.8 us -> 80.5 us (0.938)
  local copies, waits for them, and re-layouts: 9.37 us -> 0 us
  Pallas kernels: 75.4 us -> 79.7 us
    unnamed x18 -> x0, local copies, waits for them, and re-layouts: 9.37 us -> none
    pallas_call x1, Pallas kernels: 71.8 us -> 75 us  [step(): pl.pallas_call(step_kernel, out_shape=jax.ShapeDtypeStruct((TILES, 16, 12...]
    pallas_call x1, Pallas kernels: 3.6 us -> 4.73 us  [unpack(): pl.pallas_call(unpack_kernel, out_shape=[jax.ShapeDtypeStruct(shape, F32)...]
where the time goes in v4:
time: 80.5 us; the launch traced here: 80.4 us
  Pallas kernels  79.7 us (99%)
    pallas_call x1, Pallas kernels, step(): pl.pallas_call(step_kernel, out_shape=jax.ShapeDtypeStruct((TILES, 16, 12...  75 us
    pallas_call x1, Pallas kernels, unpack(): pl.pallas_call(unpack_kernel, out_shape=[jax.ShapeDtypeStruct(shape, F32)...  4.73 us

profile of v4, /device:TPU:1, one launch (start us, length us, event | category | flops | bytes accessed | tf_op | source)
XLA Modules:
  0.0 80.4 jit_solution(10082098443146575656)
XLA Ops:
  0.6 75.0 %shard_map.119.total_hbm = bf16[832,16,128]{2,1,0:T(8,128)(2,1)} custom-call(s32[5,16,128]{2,1,0:T(8,128)} %bitcast.14, s32[1,8]{1,0:T(1,128)} %bitcast.15, bf16[13,32]{1,0:T(8,128)(2,1)} %lift_ref.1, bf16[9,160,64]{2,1,0:T(8,128)(2,1)} %bitcast.12, bf16[9,64,128]{2,1,0:T(8,128)(2,1)} %bitcast.13, bf16[9,128,256]{2,1,0:T(8,128)(2,1)} %bitcast.11, ...), custom_call_target="tpu_custom_call" | custom-call | tf_op jit(solution)/shard_map/pallas_call | solution.py:343
  75.6 4.7 %shard_map.120 = (f32[9,160,64]{2,1,0:T(8,128)}, f32[9,64,128]{2,1,0:T(8,128)}, f32[9,128,256]{2,1,0:T(8,128)}, f32[9,256,512]{2,1,0:T(8,128)}, f32[512]{0:T(512)}) custom-call(bf16[832,16,128]{2,1,0:T(8,128)(2,1)} %shard_map.119.total_hbm), custom_call_target="tpu_custom_call" | custom-call | tf_op jit(solution)/shard_map/pallas_call | solution.py:720

commit v5 on v4

--- a/solution.py
+++ b/solution.py
@@ -16,11 +16,11 @@
 DEEPEST_AT, DEEPER_AT, MIDDLE_AT, TEMPORAL_AT = 0, 288, 360, 378
 HEAD_AT, HALF_ENDS = 398, (403, 399)
 PARTS = (
-    (("z", "x", "y"), False, 3),
+    (("z", "x", "y"), False, 2),
     (("x", "y", "z"), True, 1),
     (("y", "x", "z"), True, 1),
-    (("x", "y", "z"), False, 2),
-    (("y", "x", "z"), False, 2),
+    (("x", "y", "z"), False, 3),
+    (("y", "x", "z"), False, 3),
 )
 
 
@@ -69,20 +69,22 @@
     return jnp.where(index == size - 1, 0.0, rolled)
 
 
-def tap_of(ref, p, q, rows, phases):
-    a, b = p // 2, p % 2
+def tap_of(ref, p, q, rows, phases, start=0):
+    a, b = start + p // 2, p % 2
     c, d = q // 2, q % 2
     block = ref[a : a + rows, b, c : c + phases, d]
     return block.reshape(rows * phases * block.shape[2], block.shape[3])
 
 
-def store_map(ref, value, rows, phases):
+def store_map(ref, value, rows, phases, start=0):
     shifted = later(value[:, phases - 1])
-    for r in range(rows):
+    value = {start + r: value[r] for r in range(rows)}
+    shifted = {start + r: shifted[r] for r in range(rows)}
+    for r in range(start, start + rows):
         ref[r // 2, r % 2, 0, 0] = shifted[r].astype(BF)
         for m in range(phases):
             s = m + 1
-            ref[r // 2, r % 2, s // 2, s % 2] = value[r, m].astype(BF)
+            ref[r // 2, r % 2, s // 2, s % 2] = value[r][m].astype(BF)
 
 
 def map_grad(delta, weight_ref, rows, phases):
@@ -202,19 +204,23 @@
         )
     for row in range(16):
         lift_row(order, shifts, lift, occ_ref, row, None, lifted, row + 15)
+    loads[0].wait()
+
+    def first_rows(start, rows):
+        pre = jnp.zeros((64 * rows, 64), F32)
+        for p in range(3):
+            for q in range(3):
+                pre = pre + dot(tap_of(lifted, p, q, rows, 4, start), w1_ref[3 * p + q])
+        value, slope = activate(pre)
+        store_map(first, value.reshape(rows, 4, 16, 64), rows, 4, start)
+        first_slope[start : start + rows] = slope.reshape(rows, 4, 16, 64)
+
+    first_rows(8, 7)
     halo.wait_recv()
     keep = jnp.where(space == 0, 0, 1)
     for row in range(1, 16):
         lift_row(order, shifts, lift, landed, row, keep, lifted, row - 1)
-
-    loads[0].wait()
-    pre = jnp.zeros((960, 64), F32)
-    for p in range(3):
-        for q in range(3):
-            pre = pre + dot(tap_of(lifted, p, q, 15, 4), w1_ref[3 * p + q])
-    value, slope = activate(pre)
-    store_map(first, value.reshape(15, 4, 16, 64), 15, 4)
-    first_slope[...] = slope.reshape(15, 4, 16, 64)
+    first_rows(0, 8)
 
     loads[1].wait()
     pre = jnp.zeros((224, 128), F32)
@@ -266,9 +272,9 @@
         for lane in range(4):
             at = (lane // 2) * HALF + DEEPEST_AT + 32 * t + 16 * (lane % 2)
             grads_ref[at : at + 16] = grad[:, 128 * lane : 128 * lane + 128].reshape(16, 16, 128)
-        if t == 2:
+        if t == 1:
             reducing.begin(0)
-        if t == 6:
+        if t == 5:
             reducing.begin(1)
     head_grad = jnp.sum(fourth * logit_grad, axis=0, keepdims=True)
     row = lax.broadcasted_iota(jnp.int32, (16, 128), 0)
@@ -305,7 +311,6 @@
     delta = jnp.concatenate(
         [dx[(r, m)] * second_slope[r, m] for r in range(7) for m in range(2)], axis=0
     ).astype(BF)
-    reducing.advance(0)
 
     for t in range(9):
         grad = dot_tn(tap_of(first, t // 3, t % 3, 7, 2), delta).astype(BF).reshape(4, 16, 128)
@@ -319,8 +324,6 @@
             at = 64 * r + 16 * m
             first_delta[at : at + 16, :] = dx[(r, m)] * first_slope[r, m]
     first_delta[960:1024, :] = jnp.zeros((64, 64), F32)
-    reducing.advance(0)
-    reducing.advance(1)
 
     turned = jnp.transpose(first_delta[...]).astype(BF)
     for t in range(9):
@@ -329,9 +332,6 @@
         grad = jnp.concatenate([grad[0:80], grad[80:160]], axis=1).astype(BF)
         at = TEMPORAL_AT + 5 * t if t < 5 else HALF + TEMPORAL_AT + 5 * (t - 5)
         grads_ref[at : at + 5] = grad.reshape(5, 16, 128)
-        if t == 4:
-            reducing.advance(0)
-            reducing.advance(2)
     reducing.begin(3)
     reducing.begin(4)
     reducing.finish()
@@ -437,90 +437,6 @@
     return block.astype(F32)
 
 
-def relayed_scatter(wires, here, axis, parts, right_in, left_in, right_out, left_out, m):
-    n = SIZE[axis]
-    half, h = n // 2, m // 2
-    me = here[axis]
-    right, left = along(here, axis, 1), along(here, axis, -1)
-
-    def chunk(distance):
-        return lax.rem(me + distance + n, n)
-
-    lo, hi = pl.ds(0, h), pl.ds(h, m - h)
-    far = chunk(half)
-    from_left = [wires.send(parts.at[far, lo], right_in.at[0, lo], right)]
-    from_right = [wires.send(parts.at[far, hi], left_in.at[0, hi], left)]
-    early_left = wires.send(parts.at[chunk(half - 1), hi], right_in.at[1, hi], right)
-    early_right = wires.send(parts.at[chunk(1 - half), lo], left_in.at[1, lo], left)
-    for s in range(1, half):
-        yield
-        to_right, to_left = chunk(half - s), chunk(s - half)
-        if s == 1:
-            from_left[-1].wait_recv()
-            right_out[0, 0:h] = (f32(parts[to_right, 0:h]) + f32(right_in[0, 0:h])).astype(BF)
-            from_left.append(wires.send(right_out.at[0, lo], right_in.at[1, lo], right))
-            from_right[-1].wait_recv()
-            left_out[0, h:m] = (f32(parts[to_left, h:m]) + f32(left_in[0, h:m])).astype(BF)
-            from_right.append(wires.send(left_out.at[0, hi], left_in.at[1, hi], left))
-        else:
-            if s == 2:
-                early_left.wait_recv()
-                early_right.wait_recv()
-            from_left[-1].wait_recv()
-            right_out[s - 1] = (f32(parts[to_right]) + f32(right_in[s - 1])).astype(BF)
-            from_left.append(wires.send(right_out.at[s - 1], right_in.at[s], right))
-            from_right[-1].wait_recv()
-            left_out[s - 1] = (f32(parts[to_left]) + f32(left_in[s - 1])).astype(BF)
-            from_right.append(wires.send(left_out.at[s - 1], left_in.at[s], left))
-    yield
-    if half == 2:
-        early_left.wait_recv()
-        early_right.wait_recv()
-    from_left[-1].wait_recv()
-    from_right[-1].wait_recv()
-    return f32(parts[me]) + f32(right_in[half - 1]) + f32(left_in[half - 1])
-
-
-def relayed_gather(wires, here, axis, total_ref, base, m, partner):
-    n = SIZE[axis]
-    half, h = n // 2, m // 2
-    me = here[axis]
-    right, left = along(here, axis, 1), along(here, axis, -1)
-    swapped = []
-
-    def piece(distance, at, size):
-        k = lax.rem(me + distance + n, n)
-        return total_ref.at[pl.ds(base + k * m + at, size)]
-
-    def swap(where):
-        swapped.append(wires.send(where, where, partner))
-
-    own = piece(0, 0, m)
-    from_left = wires.send(own, own, right)
-    from_right = wires.send(own, own, left)
-    swap(own)
-    for s in range(1, half):
-        yield
-        from_left.wait_recv()
-        at, size = (0, h) if s == half - 1 else (0, m)
-        here_now = piece(-s, at, size)
-        from_left = wires.send(here_now, here_now, right)
-        swap(piece(-s, 0, m))
-        from_right.wait_recv()
-        at, size = (h, m - h) if s == half - 1 else (0, m)
-        here_now = piece(s, at, size)
-        from_right = wires.send(here_now, here_now, left)
-        swap(piece(s, 0, m))
-    yield
-    from_left.wait_recv()
-    swap(piece(-half, 0, h))
-    from_right.wait_recv()
-    swap(piece(half, h, m - h))
-    yield
-    for copy in swapped:
-        copy.wait_recv()
-
-
 def direct_scatter(wires, here, axis, parts, landed):
     n = SIZE[axis]
     flights = []
@@ -542,6 +458,26 @@
     flights = [wires.send(own, own, along(here, axis, d)) for d in range(1, n)]
     yield
     for copy in flights:
+        copy.wait_recv()
+
+
+def direct_gather_swap(wires, here, axis, total_ref, base, m, partner):
+    n = SIZE[axis]
+
+    def chunk(distance):
+        k = lax.rem(here[axis] + distance + n, n)
+        return total_ref.at[pl.ds(base + k * m, m)]
+
+    own = chunk(0)
+    near_first = sorted(range(1, n), key=lambda d: min(d, n - d))
+    flights = [(d, wires.send(own, own, along(here, axis, d))) for d in near_first]
+    swapped = [wires.send(own, own, partner)]
+    yield
+    for d, copy in flights:
+        copy.wait_recv()
+        swapped.append(wires.send(chunk(-d), chunk(-d), partner))
+    yield
+    for copy in swapped:
         copy.wait_recv()
 
 
@@ -567,10 +503,7 @@
     m = b * c * kept
     return [
         pltpu.VMEM((a, m, 16, 128), BF),
-        pltpu.VMEM((a // 2, m, 16, 128), BF),
-        pltpu.VMEM((a // 2, m, 16, 128), BF),
-        pltpu.VMEM((a // 2, m, 16, 128), BF),
-        pltpu.VMEM((a // 2, m, 16, 128), BF),
+        pltpu.VMEM((a - 1, m, 16, 128), BF),
         pltpu.VMEM((b, c * kept, 16, 128), BF),
         pltpu.VMEM((b - 1, c * kept, 16, 128), BF),
         pltpu.VMEM((c, kept, 16, 128), BF),
@@ -579,7 +512,7 @@
 
 
 def reduce_part(wires, here, partner, grads_ref, total_ref, paired, scratch, start, part):
-    shared, right_in, left_in, right_out, left_out, sum1, landed2, sum2, landed3 = scratch
+    shared, landed1, sum1, landed2, sum2, landed3 = scratch
     order, split, kept = part
     a, b, c = shares(order, split)
     m = b * c * kept
@@ -590,9 +523,7 @@
     flight.wait_recv()
     both = f32(grads_ref[pl.ds(core * HALF + start, a * m)]) + f32(paired[start : start + a * m])
     shared[...] = both.astype(BF).reshape(a, m, 16, 128)
-    total = yield from relayed_scatter(
-        wires, here, order[0], shared, right_in, left_in, right_out, left_out, m
-    )
+    total = yield from direct_scatter(wires, here, order[0], shared, landed1)
     sum1[...] = total.astype(BF).reshape(b, c * kept, 16, 128)
     total = yield from direct_scatter(wires, here, order[1], sum1, landed2)
     sum2[...] = total.astype(BF).reshape(c, kept, 16, 128)
@@ -609,7 +540,7 @@
     else:
         total_ref[pl.ds(base2, kept)] = total.astype(BF)
     yield from direct_gather(wires, here, order[1], total_ref, base1, c * kept)
-    yield from relayed_gather(wires, here, order[0], total_ref, base0, m, partner)
+    yield from direct_gather_swap(wires, here, order[0], total_ref, base0, m, partner)
 
 
 def interleave(programs):
@@ -633,7 +564,7 @@
         self.wires = Wires(send_sem, recv_sem)
         self.programs = []
         for i, part in enumerate(PARTS):
-            own = rest[9 * i : 9 * i + 9]
+            own = rest[6 * i : 6 * i + 6]
             self.programs.append(
                 reduce_part(
                     self.wires, here, partner, grads_ref, total_ref, paired, own, STARTS[i], part

time: 80.5 us -> 74.7 us (0.928)
  Pallas kernels: 79.7 us -> 73.9 us
    pallas_call x1, Pallas kernels: 75 us -> 69.2 us  [step(): pl.pallas_call(step_kernel, out_shape=jax.ShapeDtypeStruct((TILES, 16, 12...]
where the time goes in v5:
time: 74.7 us; the launch traced here: 74.6 us
  Pallas kernels  73.9 us (99%)
    pallas_call x1, Pallas kernels, step(): pl.pallas_call(step_kernel, out_shape=jax.ShapeDtypeStruct((TILES, 16, 12...  69.2 us
    pallas_call x1, Pallas kernels, unpack(): pl.pallas_call(unpack_kernel, out_shape=[jax.ShapeDtypeStruct(shape, F32)...  4.73 us

profile of v5, /device:TPU:1, one launch (start us, length us, event | category | flops | bytes accessed | tf_op | source)
XLA Modules:
  0.0 74.6 jit_solution(5844728866983400227)
XLA Ops:
  0.6 69.2 %shard_map.119.total_hbm = bf16[832,16,128]{2,1,0:T(8,128)(2,1)} custom-call(s32[5,16,128]{2,1,0:T(8,128)} %bitcast.14, s32[1,8]{1,0:T(1,128)} %bitcast.15, bf16[13,32]{1,0:T(8,128)(2,1)} %lift_ref.1, bf16[9,160,64]{2,1,0:T(8,128)(2,1)} %bitcast.12, bf16[9,64,128]{2,1,0:T(8,128)(2,1)} %bitcast.13, bf16[9,128,256]{2,1,0:T(8,128)(2,1)} %bitcast.11, ...), custom_call_target="tpu_custom_call" | custom-call | tf_op jit(solution)/shard_map/pallas_call | solution.py:343
  69.8 4.7 %shard_map.120 = (f32[9,160,64]{2,1,0:T(8,128)}, f32[9,64,128]{2,1,0:T(8,128)}, f32[9,128,256]{2,1,0:T(8,128)}, f32[9,256,512]{2,1,0:T(8,128)}, f32[512]{0:T(512)}) custom-call(bf16[832,16,128]{2,1,0:T(8,128)(2,1)} %shard_map.119.total_hbm), custom_call_target="tpu_custom_call" | custom-call | tf_op jit(solution)/shard_map/pallas_call | solution.py:651

commit v6 on v5

--- a/solution.py
+++ b/solution.py
@@ -317,6 +317,7 @@
         for half in range(2):
             at = half * HALF + MIDDLE_AT + 2 * t
             grads_ref[at : at + 2] = grad[2 * half : 2 * half + 2]
+    reducing.begin(3)
     reducing.advance(2)
     dx = map_grad(delta, w2_ref, 7, 2)
     for r in range(15):
@@ -332,7 +333,8 @@
         grad = jnp.concatenate([grad[0:80], grad[80:160]], axis=1).astype(BF)
         at = TEMPORAL_AT + 5 * t if t < 5 else HALF + TEMPORAL_AT + 5 * (t - 5)
         grads_ref[at : at + 5] = grad.reshape(5, 16, 128)
-    reducing.begin(3)
+        if t == 3:
+            reducing.advance(3)
     reducing.begin(4)
     reducing.finish()
     halo.wait_send()
@@ -472,8 +474,8 @@
     near_first = sorted(range(1, n), key=lambda d: min(d, n - d))
     flights = [(d, wires.send(own, own, along(here, axis, d))) for d in near_first]
     swapped = [wires.send(own, own, partner)]
-    yield
     for d, copy in flights:
+        yield
         copy.wait_recv()
         swapped.append(wires.send(chunk(-d), chunk(-d), partner))
     yield
@@ -577,7 +579,7 @@
     advance = begin
 
     def finish(self):
-        interleave(self.programs)
+        interleave([self.programs[i] for i in (4, 1, 0, 2, 3)])
         self.wires.finish()
 
 

time: 74.7 us -> 73.2 us (0.980)
  Pallas kernels: 73.9 us -> 72.4 us
    pallas_call x1, Pallas kernels: 69.2 us -> 67.7 us  [step(): pl.pallas_call(step_kernel, out_shape=jax.ShapeDtypeStruct((TILES, 16, 12...]
where the time goes in v6:
time: 73.2 us; the launch traced here: 73.1 us
  Pallas kernels  72.4 us (99%)
    pallas_call x1, Pallas kernels, step(): pl.pallas_call(step_kernel, out_shape=jax.ShapeDtypeStruct((TILES, 16, 12...  67.7 us
    pallas_call x1, Pallas kernels, unpack(): pl.pallas_call(unpack_kernel, out_shape=[jax.ShapeDtypeStruct(shape, F32)...  4.73 us

profile of v6, /device:TPU:1, one launch (start us, length us, event | category | flops | bytes accessed | tf_op | source)
XLA Modules:
  0.0 73.1 jit_solution(12501817857526475396)
XLA Ops:
  0.6 67.7 %shard_map.119.total_hbm = bf16[832,16,128]{2,1,0:T(8,128)(2,1)} custom-call(s32[5,16,128]{2,1,0:T(8,128)} %bitcast.14, s32[1,8]{1,0:T(1,128)} %bitcast.15, bf16[13,32]{1,0:T(8,128)(2,1)} %lift_ref.1, bf16[9,160,64]{2,1,0:T(8,128)(2,1)} %bitcast.12, bf16[9,64,128]{2,1,0:T(8,128)(2,1)} %bitcast.13, bf16[9,128,256]{2,1,0:T(8,128)(2,1)} %bitcast.11, ...), custom_call_target="tpu_custom_call" | custom-call | tf_op jit(solution)/shard_map/pallas_call | solution.py:345
  68.3 4.7 %shard_map.120 = (f32[9,160,64]{2,1,0:T(8,128)}, f32[9,64,128]{2,1,0:T(8,128)}, f32[9,128,256]{2,1,0:T(8,128)}, f32[9,256,512]{2,1,0:T(8,128)}, f32[512]{0:T(512)}) custom-call(bf16[832,16,128]{2,1,0:T(8,128)(2,1)} %shard_map.119.total_hbm), custom_call_target="tpu_custom_call" | custom-call | tf_op jit(solution)/shard_map/pallas_call | solution.py:653

commit v7 on v6

--- a/solution.py
+++ b/solution.py
@@ -483,6 +483,38 @@
         copy.wait_recv()
 
 
+def relayed_gather_swap(wires, here, axis, total_ref, base, m, partner):
+    n = SIZE[axis]
+    h = m // 2
+    right, left = along(here, axis, 1), along(here, axis, -1)
+
+    def piece(distance, at, size):
+        k = lax.rem(here[axis] + distance + n, n)
+        return total_ref.at[pl.ds(base + k * m + at, size)]
+
+    own, behind, ahead = (piece(distance, 0, m) for distance in (0, -1, 1))
+    from_left = wires.send(own, own, right)
+    from_right = wires.send(own, own, left)
+    swapped = [wires.send(own, own, partner)]
+    yield
+    low, high = piece(-1, 0, h), piece(1, h, m - h)
+    from_left.wait_recv()
+    far_left = wires.send(low, low, right)
+    from_right.wait_recv()
+    far_right = wires.send(high, high, left)
+    swapped += [wires.send(behind, behind, partner), wires.send(ahead, ahead, partner)]
+    yield
+    far_left.wait_recv()
+    low = piece(2, 0, h)
+    swapped.append(wires.send(low, low, partner))
+    far_right.wait_recv()
+    high = piece(2, h, m - h)
+    swapped.append(wires.send(high, high, partner))
+    yield
+    for copy in swapped:
+        copy.wait_recv()
+
+
 def direct_exchange(wires, here, axis, own, landed):
     n = SIZE[axis]
     me = here[axis]
@@ -542,7 +574,8 @@
     else:
         total_ref[pl.ds(base2, kept)] = total.astype(BF)
     yield from direct_gather(wires, here, order[1], total_ref, base1, c * kept)
-    yield from direct_gather_swap(wires, here, order[0], total_ref, base0, m, partner)
+    last = relayed_gather_swap if a == 4 else direct_gather_swap
+    yield from last(wires, here, order[0], total_ref, base0, m, partner)
 
 
 def interleave(programs):

time: 73.2 us -> 74 us (1.011)
  Pallas kernels: 72.4 us -> 73.2 us
where the time goes in v7:
time: 74 us; the launch traced here: 73.8 us
  Pallas kernels  73.2 us (99%)
    pallas_call x1, Pallas kernels, step(): pl.pallas_call(step_kernel, out_shape=jax.ShapeDtypeStruct((TILES, 16, 12...  68.4 us
    pallas_call x1, Pallas kernels, unpack(): pl.pallas_call(unpack_kernel, out_shape=[jax.ShapeDtypeStruct(shape, F32)...  4.73 us

profile of v7, /device:TPU:1, one launch (start us, length us, event | category | flops | bytes accessed | tf_op | source)
XLA Modules:
  0.0 73.8 jit_solution(14194983808224685268)
XLA Ops:
  0.6 68.4 %shard_map.119.total_hbm = bf16[832,16,128]{2,1,0:T(8,128)(2,1)} custom-call(s32[5,16,128]{2,1,0:T(8,128)} %bitcast.14, s32[1,8]{1,0:T(1,128)} %bitcast.15, bf16[13,32]{1,0:T(8,128)(2,1)} %lift_ref.1, bf16[9,160,64]{2,1,0:T(8,128)(2,1)} %bitcast.12, bf16[9,64,128]{2,1,0:T(8,128)(2,1)} %bitcast.13, bf16[9,128,256]{2,1,0:T(8,128)(2,1)} %bitcast.11, ...), custom_call_target="tpu_custom_call" | custom-call | tf_op jit(solution)/shard_map/pallas_call | solution.py:345
  69.1 4.7 %shard_map.120 = (f32[9,160,64]{2,1,0:T(8,128)}, f32[9,64,128]{2,1,0:T(8,128)}, f32[9,128,256]{2,1,0:T(8,128)}, f32[9,256,512]{2,1,0:T(8,128)}, f32[512]{0:T(512)}) custom-call(bf16[832,16,128]{2,1,0:T(8,128)(2,1)} %shard_map.119.total_hbm), custom_call_target="tpu_custom_call" | custom-call | tf_op jit(solution)/shard_map/pallas_call | solution.py:686

commit v8 on v6

--- a/solution.py
+++ b/solution.py
@@ -344,7 +344,7 @@
     hbm = pl.BlockSpec(memory_space=pl.ANY)
     return pl.pallas_call(
         step_kernel,
-        out_shape=jax.ShapeDtypeStruct((TILES, 16, 128), BF),
+        out_shape=pltpu.VMEM((TILES, 16, 128), BF),
         in_specs=[vmem()] * 3 + [hbm] * 4 + [vmem()],
         out_specs=vmem(),
         scratch_shapes=[
@@ -369,7 +369,7 @@
         ]
         + reduce_scratch(),
         compiler_params=pltpu.CompilerParams(
-            collective_id=0, has_side_effects=True, vmem_limit_bytes=67043328
+            collective_id=0, has_side_effects=True, vmem_limit_bytes=61500000
         ),
     )(occ, labels, lift, w1, w2, w3, w4, head)
 
@@ -594,17 +594,7 @@
     return scratch
 
 
-def unpack_kernel(total_hbm, g1, g2, g3, g4, gh, total_ref, s1, s2, s3, s4, load_sem, sem):
-    spans = [(32 * t, 32) for t in range(9)] + [(DEEPER_AT, HALF - DEEPER_AT)]
-    loads = []
-    for i, (at, size) in enumerate(spans):
-        for half in range(2):
-            where = pl.ds(half * HALF + at, size)
-            load = pltpu.make_async_copy(
-                total_hbm.at[where], total_ref.at[where], load_sem.at[2 * i + half]
-            )
-            load.start()
-            loads.append(load)
+def unpack_kernel(total_ref, g1, g2, g3, g4, gh, s1, s2, s3, s4, sem):
     copies = []
 
     def out(source, target):
@@ -613,16 +603,12 @@
         copies.append(copy)
 
     for t in range(9):
-        loads[2 * t].wait()
-        loads[2 * t + 1].wait()
         for lane in range(4):
             at = (lane // 2) * HALF + DEEPEST_AT + 32 * t + 16 * (lane % 2)
             s4[t, :, 128 * lane : 128 * lane + 128] = f32(
                 total_ref[at : at + 16].reshape(256, 128)
             )
         out(s4.at[t], g4.at[t])
-    loads[18].wait()
-    loads[19].wait()
     for t in range(9):
         for half in range(2):
             at = half * HALF + DEEPER_AT + 8 * t
@@ -653,12 +639,11 @@
     return pl.pallas_call(
         unpack_kernel,
         out_shape=[jax.ShapeDtypeStruct(shape, F32) for shape in shapes + ((512,),)],
-        in_specs=[hbm],
+        in_specs=[vmem()],
         out_specs=[hbm] * 4 + [vmem()],
-        scratch_shapes=[pltpu.VMEM((TILES, 16, 128), BF)]
-        + [pltpu.VMEM(shape, F32) for shape in shapes]
-        + [pltpu.SemaphoreType.DMA((20,)), pltpu.SemaphoreType.DMA((12,))],
-        compiler_params=pltpu.CompilerParams(vmem_limit_bytes=67043328),
+        scratch_shapes=[pltpu.VMEM(shape, F32) for shape in shapes]
+        + [pltpu.SemaphoreType.DMA((12,))],
+        compiler_params=pltpu.CompilerParams(vmem_limit_bytes=48000000),
     )(total)
 
 

time: 73.2 us -> 70.3 us (0.960)
  Pallas kernels: 72.4 us -> 69.5 us
    pallas_call x1, Pallas kernels: 67.7 us -> 65.9 us  [step(): pl.pallas_call(step_kernel, out_shape=pltpu.VMEM((TILES, 16, 128), BF), i...]
    pallas_call x1, Pallas kernels: 4.73 us -> 3.6 us  [unpack(): pl.pallas_call(unpack_kernel, out_shape=[jax.ShapeDtypeStruct(shape, F32)...]
where the time goes in v8:
time: 70.3 us; the launch traced here: 70.2 us
  Pallas kernels  69.5 us (99%)
    pallas_call x1, Pallas kernels, step(): pl.pallas_call(step_kernel, out_shape=pltpu.VMEM((TILES, 16, 128), BF), i...  65.9 us
    pallas_call x1, Pallas kernels, unpack(): pl.pallas_call(unpack_kernel, out_shape=[jax.ShapeDtypeStruct(shape, F32)...  3.6 us

profile of v8, /device:TPU:1, one launch (start us, length us, event | category | flops | bytes accessed | tf_op | source)
XLA Modules:
  0.0 70.2 jit_solution(7765731386967869526)
XLA Ops:
  0.6 65.9 %shard_map.119.total_ref = bf16[832,16,128]{2,1,0:T(8,128)(2,1)S(1)} custom-call(s32[5,16,128]{2,1,0:T(8,128)} %bitcast.14, s32[1,8]{1,0:T(1,128)} %bitcast.15, bf16[13,32]{1,0:T(8,128)(2,1)} %lift_ref.1, bf16[9,160,64]{2,1,0:T(8,128)(2,1)} %bitcast.12, bf16[9,64,128]{2,1,0:T(8,128)(2,1)} %bitcast.13, bf16[9,128,256]{2,1,0:T(8,128)(2,1)} %bitcast.11, ...), custom_call_target="tpu_custom_call" | custom-call | tf_op jit(solution)/shard_map/pallas_call | solution.py:345
  66.6 3.6 %shard_map.120 = (f32[9,160,64]{2,1,0:T(8,128)}, f32[9,64,128]{2,1,0:T(8,128)}, f32[9,128,256]{2,1,0:T(8,128)}, f32[9,256,512]{2,1,0:T(8,128)}, f32[512]{0:T(512)}) custom-call(bf16[832,16,128]{2,1,0:T(8,128)(2,1)S(1)} %shard_map.119.total_ref), custom_call_target="tpu_custom_call" | custom-call | tf_op jit(solution)/shard_map/pallas_call | solution.py:639
